TPU v7x, 32 devices: a whole 2x2x4 slice. The times are simulated.
32 devices in a mesh: tm: 8 (over z, core), trans: 4 (over y, x).
Axes of the slice: x: 2, y: 2, z: 4, core: 2. Of those that a mesh axis runs over, the one named last changes fastest.
Arguments:
- light_field: float32 [2, 256, 16, 1024], P(None, 'trans', 'tm'), may hold values from -6 to 6
- gas_density: float32 [256, 1024], replicated, may hold values from 0.5 to 2
- phase_x: float32 [256], replicated, may hold values from -3.140625 to 3.140625
- phase_y: float32 [1024], replicated, may hold values from -3.140625 to 3.140625
Outputs:
- light_out: float32 [2, 256, 16, 1024], P(None, 'trans', 'tm')
- electrons: float32 [256, 16, 1024], P('trans', 'tm')
All inputs are finite; a program needn't handle non-finite values.
Results may differ from a plain program's by a relative error of at most 0.0003.
Values sent between devices are 32-bit elements; how exact they have to be, the bound alone decides.
No kernel may reach another device: no remote copies, remote signals or barrier semaphores. Data moves between devices by JAX's collectives and lax.ppermute only.
A program may use at most 64 MiB of HBM per device.

v0:
```python
import functools
import math

import jax
import jax.numpy as jnp
import numpy as np
from jax import lax
from jax.experimental import pallas as pl
from jax.experimental.pallas import tpu as pltpu
from jax.sharding import Mesh
from jax.sharding import PartitionSpec as P

PHOTONS = 8
STEPS = 2
RATE_COEF = 1.8e-08
RECOMB = 0.02
KERR_COEF = 0.3
PLASMA = 4.0
LANES = 128
F32 = jnp.float32
BF16 = jnp.bfloat16
VMEM_SPEC = pl.BlockSpec(memory_space=pltpu.VMEM)
SMEM_SPEC = pl.BlockSpec(memory_space=pltpu.SMEM)


def sincos(angle):
    turns = jnp.floor(angle * (2.0 / math.pi) + 0.5)
    rest = angle - turns * 1.5703125
    rest = rest - turns * 4.837512969970703125e-4
    rest = rest - turns * 7.54978995489188e-8
    square = rest * rest
    sine = ((-1.9515295891e-4 * square + 8.3321608736e-3) * square - 1.6666654611e-1) * square
    sine = sine * rest + rest
    cosine = (2.443315711809948e-5 * square - 1.388731625493765e-3) * square
    cosine = (cosine + 4.166664568298827e-2) * (square * square) - 0.5 * square + 1.0
    quadrant = turns.astype(jnp.int32)
    odd = (quadrant & 1) == 1
    sine, cosine = jnp.where(odd, cosine, sine), jnp.where(odd, sine, cosine)
    sine = jnp.where((quadrant & 2) == 2, -sine, sine)
    cosine = jnp.where(((quadrant + 1) & 2) == 2, -cosine, cosine)
    return sine, cosine


def split3(value):
    high = value.astype(BF16)
    rest = value - high.astype(F32)
    middle = rest.astype(BF16)
    low = (rest - middle.astype(F32)).astype(BF16)
    return high, middle, low


def turned(value, order, position, sign):
    re, im = value
    eighth = (position * 8) // order
    if (position * 8) % order == 0 and eighth % 2 == 0:
        quarter = (eighth // 2 * sign) % 4
        return ((re, im), (-im, re), (-re, -im), (im, -re))[quarter]
    angle = sign * 2.0 * math.pi * position / order
    c, s = math.cos(angle), math.sin(angle)
    if (position * 8) % order == 0:
        root = math.sqrt(0.5)
        sc, ss = math.copysign(1, c), math.copysign(1, s)
        one = re - im if sc == ss else re + im
        two = re + im if sc == ss else re - im
        new_re = one * (root * sc)
        new_im = two * (root * ss) if sc == ss else two * (root * ss)
        return (new_re, new_im)
    return (re * c - im * s, re * s + im * c)


def small_dft(values, sign):
    count = len(values)
    if count == 1:
        return values
    even = small_dft(values[0::2], sign)
    odd = small_dft(values[1::2], sign)
    upper, lower = [], []
    for k in range(count // 2):
        other = turned(odd[k], count, k, sign)
        upper.append((even[k][0] + other[0], even[k][1] + other[1]))
        lower.append((even[k][0] - other[0], even[k][1] - other[1]))
    return upper + lower


def ionise(re, im, density):
    intensity = re * re + im * im
    power = intensity * intensity
    power = power * power
    rate = RATE_COEF * (power * power)
    loss = rate + RECOMB
    decay = jnp.exp(-loss)
    source = (1.0 - decay) * density * rate / loss
    return decay, source


def rotate(re, im, electrons):
    intensity = re * re + im * im
    sine, cosine = sincos(KERR_COEF * intensity - PLASMA * electrons)
    return re * cosine - im * sine, re * sine + im * cosine


def phase_tables(radix, sign):
    length = radix * LANES
    low = np.arange(LANES)
    angle = 2.0 * np.pi * (np.outer(low, low) % length) / length
    waves = np.concatenate([np.cos(angle), sign * np.sin(angle)], axis=1)
    block = 2.0 * np.pi * (np.outer(np.arange(radix), low) % radix) / radix
    turns = np.stack([np.cos(block), sign * np.sin(block)]) / length
    return waves.astype(np.float32), turns.astype(np.float32)


def toeplitz_blocks(phase, waves, turns, radix, sign):
    sine, cosine = sincos(phase)
    lane = lax.broadcasted_iota(jnp.int32, phase.shape, 1) % radix
    picked = [jnp.where(lane == k, part, 0.0) for part in (cosine, sine) for k in range(radix)]
    stacked = jnp.concatenate(picked, axis=0)
    spectrum = jnp.dot(
        stacked, waves, precision=lax.Precision.HIGHEST, preferred_element_type=F32
    )
    half = radix * radix
    row = lax.broadcasted_iota(jnp.int32, (LANES, LANES), 0)
    column = lax.broadcasted_iota(jnp.int32, (LANES, LANES), 1)
    blocks = []
    for k in range(radix):
        ours = slice(k * radix, (k + 1) * radix)
        theirs = slice(half + k * radix, half + (k + 1) * radix)
        re = spectrum[ours, :LANES] - spectrum[theirs, LANES:]
        im = spectrum[ours, LANES:] + spectrum[theirs, :LANES]
        full_re = jnp.sum(re * turns[0] - im * turns[1], axis=0, keepdims=True)
        full_im = jnp.sum(re * turns[1] + im * turns[0], axis=0, keepdims=True)
        spread_re = jnp.broadcast_to(full_re, (LANES, LANES))
        spread_im = jnp.broadcast_to(full_im, (LANES, LANES))
        rolled = (
            pltpu.roll(spread_re, 0, 1, stride=1, stride_axis=0),
            pltpu.roll(spread_im, 0, 1, stride=1, stride_axis=0),
        )
        wrapped = turned(rolled, radix, k, -sign)
        direct = column >= row
        blocks.append(
            (jnp.where(direct, rolled[0], wrapped[0]), jnp.where(direct, rolled[1], wrapped[1]))
        )
    return blocks


def store_right(table_ref, k, block):
    for part, (re, im) in enumerate(zip(split3(block[0]), split3(block[1]), strict=True)):
        base = part * 2 * LANES
        table_ref[k, base : base + LANES, :LANES] = re
        table_ref[k, base : base + LANES, LANES:] = im
        table_ref[k, base + LANES : base + 2 * LANES, :LANES] = -im
        table_ref[k, base + LANES : base + 2 * LANES, LANES:] = re


def store_left(table_ref, k, block):
    for part, (re, im) in enumerate(zip(split3(block[0]), split3(block[1]), strict=True)):
        base = part * 2 * LANES
        table_ref[k, :LANES, base : base + LANES] = re
        table_ref[k, LANES:, base : base + LANES] = im
        table_ref[k, :LANES, base + LANES : base + 2 * LANES] = -im
        table_ref[k, LANES:, base + LANES : base + 2 * LANES] = re


def forward_y(load, rows, radix, parts_ref):
    step = min(16, rows)
    for start in range(0, rows, step):
        blocks = small_dft([load(start, step, a) for a in range(radix)], -1)
        for k, (re, im) in enumerate(blocks):
            for part, (a, b) in enumerate(zip(split3(re), split3(im), strict=True)):
                parts_ref[k, part, start : start + step, :LANES] = a
                parts_ref[k, part, start : start + step, LANES:] = b


def product_y(parts_ref, table_ref, out_ref, radix):
    for k in range(radix):
        high, middle, low = parts_ref[k, 0], parts_ref[k, 1], parts_ref[k, 2]
        left = jnp.concatenate([high, high, high, middle, middle, low], axis=1)
        table = table_ref[k]
        right = jnp.concatenate([table, table[: 4 * LANES], table[: 2 * LANES]], axis=0)
        out_ref[k] = jnp.dot(left, right, preferred_element_type=F32)


def backward_y(out_ref, start, step, radix):
    picked = [
        (out_ref[k, start : start + step, :LANES], out_ref[k, start : start + step, LANES:])
        for k in range(radix)
    ]
    return small_dft(picked, 1)


def first_kernel(light_ref, phase_ref, waves_ref, turns_ref, send_ref, table_ref, parts_ref, mid_ref):
    radix = table_ref.shape[0]
    slabs, _, times, across, width = send_ref.shape
    blocks = toeplitz_blocks(phase_ref[...], waves_ref[...], turns_ref[...], radix, 1)
    for k, block in enumerate(blocks):
        store_right(table_ref, k, block)

    def load(start, step, a):
        t, x = start // across, start % across
        lanes = slice(a * LANES, (a + 1) * LANES)
        return light_ref[0, t, x : x + step, lanes], light_ref[1, t, x : x + step, lanes]

    forward_y(load, times * across, radix, parts_ref)
    product_y(parts_ref, table_ref, mid_ref, radix)
    for start in range(0, times * across, 8):
        t, x = start // across, start % across
        for a, pair in enumerate(backward_y(mid_ref, start, 8, radix)):
            for c in range(2):
                if width >= LANES:
                    slab, offset = a * LANES // width, a * LANES % width
                    send_ref[slab, c, t, x : x + 8, offset : offset + LANES] = pair[c]
                else:
                    for piece in range(LANES // width):
                        slab = a * LANES // width + piece
                        send_ref[slab, c, t, x : x + 8, :] = pair[c][
                            :, piece * width : (piece + 1) * width
                        ]


def table_x_kernel(phase_ref, waves_ref, turns_ref, table_ref):
    radix = table_ref.shape[0]
    blocks = toeplitz_blocks(phase_ref[...], waves_ref[...], turns_ref[...], radix, -1)
    for k, block in enumerate(blocks):
        store_left(table_ref, k, block)


def put_x(parts_ref, lanes, start, values):
    step = values[0][0].shape[0]
    for k, (re, im) in enumerate(small_dft(values, -1)):
        for part, (a, b) in enumerate(zip(split3(re), split3(im), strict=True)):
            base = part * 2 * LANES
            parts_ref[k, base + start : base + start + step, lanes] = a
            parts_ref[k, base + LANES + start : base + LANES + start + step, lanes] = b


def product_x(parts_ref, table_ref, out_ref, radix):
    for k in range(radix):
        table = table_ref[k]
        left = jnp.concatenate([table, table[:, : 4 * LANES], table[:, : 2 * LANES]], axis=1)
        high = parts_ref[k, : 2 * LANES]
        middle = parts_ref[k, 2 * LANES : 4 * LANES]
        low = parts_ref[k, 4 * LANES :]
        right = jnp.concatenate([high, high, high, middle, middle, low], axis=0)
        out_ref[k] = jnp.dot(left, right, preferred_element_type=F32)


def get_x(out_ref, lanes, start, step, radix):
    picked = [
        (out_ref[k, start : start + step, lanes], out_ref[k, LANES + start : LANES + start + step, lanes])
        for k in range(radix)
    ]
    return small_dft(picked, 1)


def second_kernel(
    recv_ref, table_ref, density_ref, field_ref, growth_ref, gained_ref, last_growth_ref, last_gained_ref,
    parts_ref, mid_ref,
):
    radix = table_ref.shape[0]
    sources, _, times, across, width = recv_ref.shape
    trans = (radix * LANES) // across
    step = min(16, across)
    total = (sources // trans) * times

    def at(c, t, x):
        core, inner = t // times, t % times
        return recv_ref[core * trans + x // across, c, inner, x % across : x % across + step, :]

    for t in range(total):
        lanes = slice(t * width, (t + 1) * width)
        for start in range(0, LANES, step):
            values = [
                (at(0, t, a * LANES + start), at(1, t, a * LANES + start)) for a in range(radix)
            ]
            put_x(parts_ref, lanes, start, values)
    product_x(parts_ref, table_ref, mid_ref, radix)
    for start in range(0, LANES, 8):
        growth, gained = [None] * radix, [None] * radix
        for t in range(total):
            lanes = slice(t * width, (t + 1) * width)
            for a, (re, im) in enumerate(get_x(mid_ref, lanes, start, 8, radix)):
                rows = slice(a * LANES + start, a * LANES + start + 8)
                field_ref[0, t, rows, :] = re
                field_ref[1, t, rows, :] = im
                decay, source = ionise(re, im, density_ref[rows, :])
                if t == 0:
                    growth[a], gained[a] = decay, source
                else:
                    gained[a] = decay * gained[a] + source
                    growth[a] = growth[a] * decay
                growth_ref[t, rows, :] = growth[a]
                gained_ref[t, rows, :] = gained[a]
                if t == total - 1:
                    last_growth_ref[rows, :] = growth[a]
                    last_gained_ref[rows, :] = gained[a]


def third_kernel(
    field_ref, growth_ref, gained_ref, entering_ref, table_ref, send_ref, parts_ref, mid_ref
):
    radix = table_ref.shape[0]
    _, total, _, width = field_ref.shape
    slabs, _, times, across, _ = send_ref.shape
    trans = (radix * LANES) // across
    for t in range(total):
        lanes = slice(t * width, (t + 1) * width)
        for start in range(0, LANES, 16):
            values = []
            for a in range(radix):
                rows = slice(a * LANES + start, a * LANES + start + 16)
                electrons = growth_ref[t, rows, :] * entering_ref[rows, :] + gained_ref[t, rows, :]
                values.append(rotate(field_ref[0, t, rows, :], field_ref[1, t, rows, :], electrons))
            put_x(parts_ref, lanes, start, values)
    product_x(parts_ref, table_ref, mid_ref, radix)
    for t in range(total):
        lanes = slice(t * width, (t + 1) * width)
        for start in range(0, LANES, 8):
            for a, pair in enumerate(get_x(mid_ref, lanes, start, 8, radix)):
                x = a * LANES + start
                slab = (t // times) * trans + x // across
                row = x % across
                for c in range(2):
                    send_ref[slab, c, t % times, row : row + 8, :] = pair[c]


def fourth_kernel(
    core_ref, recv_ref, table_ref, density_ref, field_ref, growth_ref, gained_ref, mine_ref, theirs_ref,
    parts_ref, mid_ref,
):
    radix = table_ref.shape[0]
    slabs, _, times, across, width = recv_ref.shape
    core = core_ref[0]

    def part(c, t, x, step, a):
        if width >= LANES:
            slab, offset = a * LANES // width, a * LANES % width
            return recv_ref[slab, c, t, x : x + step, offset : offset + LANES]
        pieces = LANES // width
        return jnp.concatenate(
            [recv_ref[a * pieces + p, c, t, x : x + step, :] for p in range(pieces)], axis=1
        )

    def load(start, step, a):
        t, x = start // across, start % across
        return part(0, t, x, step, a), part(1, t, x, step, a)

    forward_y(load, times * across, radix, parts_ref)
    product_y(parts_ref, table_ref, mid_ref, radix)
    half = across // 2
    for x in range(0, across, 8):
        growth, gained = [None] * radix, [None] * radix
        for t in range(times):
            for a, (re, im) in enumerate(backward_y(mid_ref, t * across + x, 8, radix)):
                lanes = slice(a * LANES, (a + 1) * LANES)
                field_ref[0, t, x : x + 8, lanes] = re
                field_ref[1, t, x : x + 8, lanes] = im
                decay, source = ionise(re, im, density_ref[x : x + 8, lanes])
                if t == 0:
                    growth[a], gained[a] = decay, source
                else:
                    gained[a] = decay * gained[a] + source
                    growth[a] = growth[a] * decay
                growth_ref[t, x : x + 8, lanes] = growth[a]
                gained_ref[t, x : x + 8, lanes] = gained[a]
    last = times - 1

    def hand_out(own):
        kept, given = slice(own * half, (own + 1) * half), slice((1 - own) * half, (2 - own) * half)
        mine_ref[0] = growth_ref[last, kept, :]
        mine_ref[1] = gained_ref[last, kept, :]
        theirs_ref[0] = growth_ref[last, given, :]
        theirs_ref[1] = gained_ref[last, given, :]

    pl.when(core == 0)(functools.partial(hand_out, 0))
    pl.when(core == 1)(functools.partial(hand_out, 1))


def fifth_kernel(core_ref, field_ref, growth_ref, gained_ref, kept_ref, given_ref, light_ref, electrons_ref):
    _, times, across, length = field_ref.shape
    half = across // 2
    core = core_ref[0]
    for x in range(0, across, 8):
        own, row = x // half, x % half
        entering = jnp.where(core == own, kept_ref[row : row + 8, :], given_ref[row : row + 8, :])
        for t in range(times):
            for a in range(length // LANES):
                lanes = slice(a * LANES, (a + 1) * LANES)
                electrons = (
                    growth_ref[t, x : x + 8, lanes] * entering[:, lanes]
                    + gained_ref[t, x : x + 8, lanes]
                )
                re, im = rotate(
                    field_ref[0, t, x : x + 8, lanes], field_ref[1, t, x : x + 8, lanes], electrons
                )
                light_ref[0, t, x : x + 8, lanes] = re
                light_ref[1, t, x : x + 8, lanes] = im
                electrons_ref[t, x : x + 8, lanes] = electrons


def call(kernel, outs, scratch, *operands, scalars=0):
    return pl.pallas_call(
        kernel,
        out_shape=[jax.ShapeDtypeStruct(shape, kind) for shape, kind in outs],
        in_specs=[SMEM_SPEC] * scalars + [VMEM_SPEC] * (len(operands) - scalars),
        out_specs=[VMEM_SPEC] * len(outs),
        scratch_shapes=[pltpu.VMEM(shape, kind) for shape, kind in scratch],
    )(*operands)


def entering_chip(growth, gained):
    count = lax.axis_size("z")
    place = lax.axis_index("z")
    before_growth = before_gained = None
    size = 1
    while size < count:
        got_growth = jnp.zeros_like(growth)
        got_gained = jnp.zeros_like(gained)
        need_growth = 2 * size < count
        for reach in range(1, size + 1):
            pairs = [
                (b + size - 1, b + size - 1 + reach)
                for b in range(0, count, 2 * size)
                if b + size - 1 + reach < count
            ]
            got_gained = got_gained + lax.ppermute(gained, "z", pairs)
            if need_growth:
                later = [pair for pair in pairs if pair[0] >= 2 * size]
                got_growth = got_growth + lax.ppermute(growth, "z", later)
        upper = (place // size) % 2 == 1
        if before_gained is None:
            new_gained, new_growth = got_gained, got_growth
            before_gained = jnp.zeros_like(gained)
            before_growth = jnp.ones_like(growth)
        else:
            new_gained = before_growth * got_gained + before_gained
            new_growth = before_growth * got_growth
        before_gained = jnp.where(upper, new_gained, before_gained)
        if need_growth:
            before_growth = jnp.where(upper, new_growth, before_growth)
            gained, growth = (
                jnp.where(upper, growth * got_gained + gained, gained),
                jnp.where(upper, growth * got_growth, growth),
            )
        size *= 2
    return jnp.zeros_like(gained) if before_gained is None else before_gained


def local(light_field, gas_density, phase_x, phase_y):
    width_x, width_y = phase_x.shape[0], phase_y.shape[0]
    radix_x, radix_y = width_x // LANES, width_y // LANES
    _, across, times, _ = light_field.shape
    trans, cores = lax.axis_size("trans"), lax.axis_size("core")
    slabs = trans * cores
    width = width_y // slabs
    total = times * cores
    slab = lax.axis_index("core") * trans + lax.axis_index("trans")
    core = lax.axis_index("core").astype(jnp.int32).reshape(1)
    density_y = lax.dynamic_slice_in_dim(gas_density, slab * width, width, 1)
    density_x = lax.dynamic_slice_in_dim(gas_density, lax.axis_index("trans") * across, across, 0)
    packed = (slabs, 2, times, across, width)
    rows = times * across

    waves_y, turns_y = phase_tables(radix_y, 1)
    waves_x, turns_x = phase_tables(radix_x, -1)
    scratch_y = [((radix_y, 3, rows, 2 * LANES), BF16), ((radix_y, rows, 2 * LANES), F32)]
    scratch_x = [
        ((radix_x, 6 * LANES, total * width), BF16),
        ((radix_x, 2 * LANES, total * width), F32),
    ]
    (table_x,) = call(
        table_x_kernel,
        [((radix_x, 2 * LANES, 6 * LANES), BF16)],
        [],
        phase_x.reshape(radix_x, LANES),
        waves_x,
        turns_x,
    )
    sent, table_y = call(
        first_kernel,
        [(packed, F32), ((radix_y, 6 * LANES, 2 * LANES), BF16)],
        scratch_y,
        light_field.transpose(0, 2, 1, 3),
        phase_y.reshape(radix_y, LANES),
        waves_y,
        turns_y,
    )
    received = lax.all_to_all(sent, ("core", "trans"), 0, 0, tiled=True)
    cells = (width_x, width)
    field, growth, gained, last_growth, last_gained = call(
        second_kernel,
        [((2, total) + cells, F32), ((total,) + cells, F32), ((total,) + cells, F32), (cells, F32), (cells, F32)],
        scratch_x,
        received,
        table_x,
        density_y,
    )
    entering = entering_chip(last_growth, last_gained)
    (sent,) = call(
        third_kernel, [(packed, F32)], scratch_x, field, growth, gained, entering, table_x
    )
    received = lax.all_to_all(sent, ("core", "trans"), 0, 0, tiled=True)
    cells = (across, width_y)
    half = (2, across // 2, width_y)
    field, growth, gained, mine, theirs = call(
        fourth_kernel,
        [((2, times) + cells, F32), ((times,) + cells, F32), ((times,) + cells, F32), (half, F32), (half, F32)],
        scratch_y,
        core,
        received,
        table_y,
        density_x,
        scalars=1,
    )
    swap = [(0, 1), (1, 0)]
    other = lax.ppermute(theirs, "core", swap)
    first = core[0] == 0
    early = jnp.where(first, mine, other)
    late = jnp.where(first, other, mine)
    entering = entering_chip(late[0] * early[0], late[0] * early[1] + late[1])
    halfway = early[0] * entering + early[1]
    kept = jnp.where(first, entering, halfway)
    given = lax.ppermute(jnp.where(first, halfway, entering), "core", swap)
    light, electrons = call(
        fifth_kernel,
        [((2, times) + cells, F32), ((times,) + cells, F32)],
        [],
        core,
        field,
        growth,
        gained,
        kept,
        given,
        scalars=1,
    )
    return light.transpose(0, 2, 1, 3), electrons.transpose(1, 0, 2)


def solution(mesh):
    count = mesh.shape["tm"]
    split = Mesh(
        mesh.devices.reshape(count // 2, 2, mesh.shape["trans"]), ("z", "core", "trans")
    )
    placed = (P(None, "trans", ("z", "core"), None), P(), P(), P())
    return jax.shard_map(
        local,
        mesh=split,
        in_specs=placed,
        out_specs=(P(None, "trans", ("z", "core"), None), P("trans", ("z", "core"), None)),
        check_vma=False,
    )
```

profile of v0, /device:TPU:17, one launch (start us, length us, event | category | flops | bytes accessed | tf_op | source)
XLA Modules:
  0.0 111.7 jit_solution(11863898938584132842)
XLA Ops:
  0.6 0.0 copy-start
  0.6 2.6 %copy.14 = f32[2,64,2,1024]{3,1,2,0:T(8,128)} copy(f32[2,64,2,1024]{3,2,1,0:T(2,128)} %param.8) | data formatting | bytes 2097152 | tf_op args[0]
  3.2 4.2 %shard_map.95 = (f32[8,2,2,64,128]{4,3,2,1,0:T(8,128)}, bf16[8,768,256]{2,1,0:T(8,128)(2,1)}) custom-call(f32[2,2,64,1024]{3,2,1,0:T(8,128)} %bitcast.40, f32[8,128]{1,0:T(8,128)} %bitcast.43, f32[128,256]{1,0:T(8,128)} %constant.84.clone.waves_ref, f32[2,8,128]{2,1,0:T(8,128)} %constant.85.clone.turns_ref), custom_call_target="tpu_custom_call" | custom-call | tf_op jit(solution)/shard_map/pallas_call | solution.py:400
  7.5 4.4 %all-to-all-start = ((f32[8,2,2,64,128]{4,3,2,1,0:T(8,128)}), f32[8,2,2,64,128]{4,3,2,1,0:T(8,128)S(1)}, u32[]{:S(2)}, u32[]{:S(2)}) async-start(f32[8,2,2,64,128]{4,3,2,1,0:T(8,128)} %get-tuple-element.16), calls=%async_computation | async-start | bytes 2097152 | tf_op jit(solution)/shard_map/all_to_all | solution.py:486
  11.9 2.2 %shard_map.96.table_ref = bf16[2,256,768]{2,1,0:T(8,128)(2,1)} custom-call(f32[2,128]{1,0:T(2,128)} %bitcast.44, f32[128,256]{1,0:T(8,128)} %constant.82.clone.waves_ref, f32[2,2,128]{2,1,0:T(2,128)} %constant.83.clone.turns_ref), custom_call_target="tpu_custom_call" | custom-call | tf_op jit(solution)/shard_map/pallas_call | solution.py:400
  14.0 0.0 copy-done
  14.0 0.7 constant_dynamic-slice_fusion.1.density_ref
  14.7 11.8 %all-to-all-done.recv_ref = f32[8,2,2,64,128]{4,3,2,1,0:T(8,128)S(1)} async-done(((f32[8,2,2,64,128]{4,3,2,1,0:T(8,128)}), f32[8,2,2,64,128]{4,3,2,1,0:T(8,128)S(1)}, u32[]{:S(2)}, u32[]{:S(2)}) %all-to-all-start) | async-done | bytes 1048608 | tf_op jit(solution)/shard_map/all_to_all | solution.py:486
  26.5 0.0 copy-start.2
  26.5 1.0 copy-done.2
  27.5 4.3 %shard_map.97 = (f32[2,4,256,128]{3,2,1,0:T(8,128)}, f32[4,256,128]{2,1,0:T(8,128)}, f32[4,256,128]{2,1,0:T(8,128)}, f32[256,128]{1,0:T(8,128)}, f32[256,128]{1,0:T(8,128)}) custom-call(f32[8,2,2,64,128]{4,3,2,1,0:T(8,128)} %copy-done.2, bf16[2,256,768]{2,1,0:T(8,128)(2,1)} %shard_map.96.table_ref, f32[256,128]{1,0:T(8,128)} %constant_dynamic-slice_fusion.1.density_ref), custom_call_target="tpu_custom_call" | custom-call | tf_op jit(solution)/shard_map/pallas_call | solution.py:400
  31.7 3.2 %collective-permute-start.1 = (f32[256,128]{1,0:T(8,128)}, f32[256,128]{1,0:T(8,128)S(1)}, u32[]{:S(2)}, u32[]{:S(2)}) collective-permute-start(f32[256,128]{1,0:T(8,128)} %get-tuple-element.21), channel_id=1, source_target_pairs={{0,8},{16,24},{1,9},{17,25},{2,10},{18,26},{3,11},{19,27},{4,12},{... | collective-permute-start | bytes 393224 | tf_op jit(solution)/shard_map/ppermute | solution.py:424
  34.9 1.3 %collective-permute-start = (f32[256,128]{1,0:T(8,128)}, f32[256,128]{1,0:T(8,128)S(1)}, u32[]{:S(2)}, u32[]{:S(2)}) collective-permute-start(f32[256,128]{1,0:T(8,128)} %get-tuple-element.20), channel_id=1, source_target_pairs={{16,24},{17,25},{18,26},{19,27},{20,28},{21,29},{22,30},{23,31}} | collective-permute-start | bytes 393224 | tf_op jit(solution)/shard_map/ppermute | solution.py:427
  36.3 1.7 %collective-permute-done.1 = f32[256,128]{1,0:T(8,128)S(1)} collective-permute-done((f32[256,128]{1,0:T(8,128)}, f32[256,128]{1,0:T(8,128)S(1)}, u32[]{:S(2)}, u32[]{:S(2)}) %collective-permute-start.1) | collective-permute-done | bytes 131104 | tf_op jit(solution)/shard_map/ppermute | solution.py:424
  38.0 1.0 add_select_fusion.3
  39.0 1.3 %collective-permute-start.2 = (f32[256,128]{1,0:T(8,128)S(1)}, f32[256,128]{1,0:T(8,128)S(1)}, u32[]{:S(2)}, u32[]{:S(2)}) collective-permute-start(f32[256,128]{1,0:T(8,128)S(1)} %add_select_fusion.3), channel_id=1, source_target_pairs={{8,16},{9,17},{10,18},{11,19},{12,20},{13,21},{14,22},{15,23}} | collective-permute-start | bytes 393224 | tf_op jit(solution)/shard_map/ppermute | solution.py:424
  40.3 0.7 collective-permute-start.3
  41.0 0.0 collective-permute-done
  41.0 3.7 %collective-permute-done.2 = f32[256,128]{1,0:T(8,128)S(1)} collective-permute-done((f32[256,128]{1,0:T(8,128)S(1)}, f32[256,128]{1,0:T(8,128)S(1)}, u32[]{:S(2)}, u32[]{:S(2)}) %collective-permute-start.2) | collective-permute-done | bytes 131104 | tf_op jit(solution)/shard_map/ppermute | solution.py:424
  44.7 0.0 collective-permute-done.3
  44.7 0.7 add_select_fusion.2.entering_ref
  45.4 4.8 %shard_map.98 = f32[8,2,2,64,128]{4,3,2,1,0:T(8,128)} custom-call(f32[2,4,256,128]{3,2,1,0:T(8,128)} %get-tuple-element.17.field_ref, f32[4,256,128]{2,1,0:T(8,128)} %get-tuple-element.18.growth_ref, f32[4,256,128]{2,1,0:T(8,128)} %get-tuple-element.19.gained_ref, f32[256,128]{1,0:T(8,128)} %add_select_fusion.2.entering_ref, ...), custom_call_target="tpu_custom_call" | custom-call | tf_op jit(solution)/shard_map/pallas_call | solution.py:400
  50.2 7.1 %all-to-all-start.1 = ((f32[8,2,2,64,128]{4,3,2,1,0:T(8,128)}), f32[8,2,2,64,128]{4,3,2,1,0:T(8,128)S(1)}, u32[]{:S(2)}, u32[]{:S(2)}) async-start(f32[8,2,2,64,128]{4,3,2,1,0:T(8,128)} %shard_map.98), calls=%async_computation.1 | async-start | bytes 2097152 | tf_op jit(solution)/shard_map/all_to_all | solution.py:500
  57.2 0.7 constant_dynamic-slice_fusion.density_ref
  58.0 13.9 %all-to-all-done.1.recv_ref = f32[8,2,2,64,128]{4,3,2,1,0:T(8,128)S(1)} async-done(((f32[8,2,2,64,128]{4,3,2,1,0:T(8,128)}), f32[8,2,2,64,128]{4,3,2,1,0:T(8,128)S(1)}, u32[]{:S(2)}, u32[]{:S(2)}) %all-to-all-start.1) | async-done | bytes 1048608 | tf_op jit(solution)/shard_map/all_to_all | solution.py:500
  71.9 0.0 copy-start.1
  71.9 1.0 copy-done.1
  72.9 5.2 %shard_map.99 = (f32[2,2,64,1024]{3,2,1,0:T(8,128)}, f32[2,64,1024]{2,1,0:T(8,128)}, f32[2,64,1024]{2,1,0:T(8,128)}, f32[2,32,1024]{2,1,0:T(8,128)}, f32[2,32,1024]{2,1,0:T(8,128)}) custom-call(s32[1]{0:T(128)} %bitcast.core_ref, f32[8,2,2,64,128]{4,3,2,1,0:T(8,128)} %copy-done.1, bf16[8,768,256]{2,1,0:T(8,128)(2,1)} %get-tuple-element.22.table_ref, ...), custom_call_target="tpu_custom_call" | custom-call | tf_op jit(solution)/shard_map/pallas_call | solution.py:400
  78.1 0.1 collective-permute-start.4
  78.2 1.6 %collective-permute-done.4 = f32[2,32,1024]{2,1,0:T(8,128)S(1)} collective-permute-done((f32[2,32,1024]{2,1,0:T(8,128)}, f32[2,32,1024]{2,1,0:T(8,128)S(1)}, u32[]{:S(2)}, u32[]{:S(2)}) %collective-permute-start.4) | collective-permute-done | bytes 262176 | tf_op jit(solution)/shard_map/ppermute | solution.py:514
  79.8 1.0 broadcast_select_fusion.1
  80.9 5.0 %collective-permute-start.6 = (f32[32,1024]{1,0:T(8,128)S(1)}, f32[32,1024]{1,0:T(8,128)S(1)}, u32[]{:S(2)}, u32[]{:S(2)}) collective-permute-start(f32[32,1024]{1,0:T(8,128)S(1)} %fusion), channel_id=1, source_target_pairs={{0,8},{16,24},{1,9},{17,25},{2,10},{18,26},{3,11},{19,27},{4,12},{... | collective-permute-start | bytes 393224 | tf_op jit(solution)/shard_map/ppermute | solution.py:424
  85.9 2.7 %collective-permute-done.6 = f32[32,1024]{1,0:T(8,128)S(1)} collective-permute-done((f32[32,1024]{1,0:T(8,128)S(1)}, f32[32,1024]{1,0:T(8,128)S(1)}, u32[]{:S(2)}, u32[]{:S(2)}) %collective-permute-start.6) | collective-permute-done | bytes 131104 | tf_op jit(solution)/shard_map/ppermute | solution.py:424
  88.6 1.3 %collective-permute-start.7 = (f32[32,1024]{1,0:T(8,128)S(1)}, f32[32,1024]{1,0:T(8,128)S(1)}, u32[]{:S(2)}, u32[]{:S(2)}) collective-permute-start(f32[32,1024]{1,0:T(8,128)S(1)} %get-tuple-element.34), channel_id=1, source_target_pairs={{8,16},{9,17},{10,18},{11,19},{12,20},{13,21},{14,22},{15,23}} | collective-permute-start | bytes 393224 | tf_op jit(solution)/shard_map/ppermute | solution.py:424
  89.9 0.7 collective-permute-start.8
  90.6 4.1 %collective-permute-start.5 = (f32[32,1024]{1,0:T(8,128)S(1)}, f32[32,1024]{1,0:T(8,128)S(1)}, u32[]{:S(2)}, u32[]{:S(2)}) collective-permute-start(f32[32,1024]{1,0:T(8,128)S(1)} %get-tuple-element.35), channel_id=1, source_target_pairs={{16,24},{17,25},{18,26},{19,27},{20,28},{21,29},{22,30},{23,31}} | collective-permute-start | bytes 393224 | tf_op jit(solution)/shard_map/ppermute | solution.py:427
  94.7 0.0 collective-permute-done.7
  94.7 0.0 collective-permute-done.8
  94.7 5.7 %collective-permute-done.5 = f32[32,1024]{1,0:T(8,128)S(1)} collective-permute-done((f32[32,1024]{1,0:T(8,128)S(1)}, f32[32,1024]{1,0:T(8,128)S(1)}, u32[]{:S(2)}, u32[]{:S(2)}) %collective-permute-start.5) | collective-permute-done | bytes 131104 | tf_op jit(solution)/shard_map/ppermute | solution.py:427
  100.5 0.6 collective-permute-start.9
  101.1 0.7 fusion.3.kept_ref
  101.8 0.3 collective-permute-done.9.given_ref
  102.1 0.0 copy-start.3
  102.1 0.7 copy-done.3
  102.8 3.7 %shard_map.100 = (f32[2,2,64,1024]{3,2,1,0:T(8,128)}, f32[2,64,1024]{2,1,0:T(8,128)}) custom-call(s32[1]{0:T(128)} %bitcast.core_ref, f32[2,2,64,1024]{3,2,1,0:T(8,128)} %get-tuple-element.23.field_ref, f32[2,64,1024]{2,1,0:T(8,128)} %get-tuple-element.24.growth_ref, f32[2,64,1024]{2,1,0:T(8,128)} %get-tuple-element.25.gained_ref, ...), custom_call_target="tpu_custom_call" | custom-call | tf_op jit(solution)/shard_map/pallas_call | solution.py:400
  106.4 3.0 %copy.11 = f32[2,64,2,1024]{3,2,1,0:T(2,128)} copy(f32[2,64,2,1024]{3,1,2,0:T(8,128)} %bitcast.41) | data formatting | bytes 2097152
  109.4 2.2 %copy.12 = f32[64,2,1024]{2,1,0:T(2,128)} copy(f32[64,2,1024]{2,0,1:T(8,128)} %bitcast.42) | data formatting | bytes 1048576
  (3 shorter events, 0.1 us)
Async XLA Ops:
  0.6 13.4 %copy-start = (f32[256,1024]{1,0:T(8,128)S(1)}, f32[256,1024]{1,0:T(8,128)}, u32[]{:S(2)}) copy-start(f32[256,1024]{1,0:T(8,128)} %param.9) | copy-start | bytes 3145732
  7.5 19.0 %all-to-all-start = ((f32[8,2,2,64,128]{4,3,2,1,0:T(8,128)}), f32[8,2,2,64,128]{4,3,2,1,0:T(8,128)S(1)}, u32[]{:S(2)}, u32[]{:S(2)}) async-start(f32[8,2,2,64,128]{4,3,2,1,0:T(8,128)} %get-tuple-element.16), calls=%async_computation | async-start | bytes 2097152 | tf_op jit(solution)/shard_map/all_to_all | solution.py:486
  26.5 1.0 copy-start.2
  31.7 6.2 %collective-permute-start.1 = (f32[256,128]{1,0:T(8,128)}, f32[256,128]{1,0:T(8,128)S(1)}, u32[]{:S(2)}, u32[]{:S(2)}) collective-permute-start(f32[256,128]{1,0:T(8,128)} %get-tuple-element.21), channel_id=1, source_target_pairs={{0,8},{16,24},{1,9},{17,25},{2,10},{18,26},{3,11},{19,27},{4,12},{... | collective-permute-start | bytes 393224 | tf_op jit(solution)/shard_map/ppermute | solution.py:424
  34.9 6.0 %collective-permute-start = (f32[256,128]{1,0:T(8,128)}, f32[256,128]{1,0:T(8,128)S(1)}, u32[]{:S(2)}, u32[]{:S(2)}) collective-permute-start(f32[256,128]{1,0:T(8,128)} %get-tuple-element.20), channel_id=1, source_target_pairs={{16,24},{17,25},{18,26},{19,27},{20,28},{21,29},{22,30},{23,31}} | collective-permute-start | bytes 393224 | tf_op jit(solution)/shard_map/ppermute | solution.py:427
  39.0 5.7 %collective-permute-start.2 = (f32[256,128]{1,0:T(8,128)S(1)}, f32[256,128]{1,0:T(8,128)S(1)}, u32[]{:S(2)}, u32[]{:S(2)}) collective-permute-start(f32[256,128]{1,0:T(8,128)S(1)} %add_select_fusion.3), channel_id=1, source_target_pairs={{8,16},{9,17},{10,18},{11,19},{12,20},{13,21},{14,22},{15,23}} | collective-permute-start | bytes 393224 | tf_op jit(solution)/shard_map/ppermute | solution.py:424
  40.3 4.4 %collective-permute-start.3 = (f32[256,128]{1,0:T(8,128)S(1)}, f32[256,128]{1,0:T(8,128)S(1)}, u32[]{:S(2)}, u32[]{:S(2)}) collective-permute-start(f32[256,128]{1,0:T(8,128)S(1)} %add_select_fusion.3), channel_id=1, source_target_pairs={{8,24},{9,25},{10,26},{11,27},{12,28},{13,29},{14,30},{15,31}} | collective-permute-start | bytes 393224 | tf_op jit(solution)/shard_map/ppermute | solution.py:424
  50.2 21.7 %all-to-all-start.1 = ((f32[8,2,2,64,128]{4,3,2,1,0:T(8,128)}), f32[8,2,2,64,128]{4,3,2,1,0:T(8,128)S(1)}, u32[]{:S(2)}, u32[]{:S(2)}) async-start(f32[8,2,2,64,128]{4,3,2,1,0:T(8,128)} %shard_map.98), calls=%async_computation.1 | async-start | bytes 2097152 | tf_op jit(solution)/shard_map/all_to_all | solution.py:500
  71.9 1.0 copy-start.1
  78.1 1.7 %collective-permute-start.4 = (f32[2,32,1024]{2,1,0:T(8,128)}, f32[2,32,1024]{2,1,0:T(8,128)S(1)}, u32[]{:S(2)}, u32[]{:S(2)}) collective-permute-start(f32[2,32,1024]{2,1,0:T(8,128)} %get-tuple-element.26), channel_id=1, source_target_pairs={{0,4},{4,0},{1,5},{5,1},{2,6},{6,2},{3,7},{7,3},{8,12},{12,8},{9,1... | collective-permute-start | bytes 786440 | tf_op jit(solution)/shard_map/ppermute | solution.py:514
  80.9 7.7 %collective-permute-start.6 = (f32[32,1024]{1,0:T(8,128)S(1)}, f32[32,1024]{1,0:T(8,128)S(1)}, u32[]{:S(2)}, u32[]{:S(2)}) collective-permute-start(f32[32,1024]{1,0:T(8,128)S(1)} %fusion), channel_id=1, source_target_pairs={{0,8},{16,24},{1,9},{17,25},{2,10},{18,26},{3,11},{19,27},{4,12},{... | collective-permute-start | bytes 393224 | tf_op jit(solution)/shard_map/ppermute | solution.py:424
  88.6 6.1 %collective-permute-start.7 = (f32[32,1024]{1,0:T(8,128)S(1)}, f32[32,1024]{1,0:T(8,128)S(1)}, u32[]{:S(2)}, u32[]{:S(2)}) collective-permute-start(f32[32,1024]{1,0:T(8,128)S(1)} %get-tuple-element.34), channel_id=1, source_target_pairs={{8,16},{9,17},{10,18},{11,19},{12,20},{13,21},{14,22},{15,23}} | collective-permute-start | bytes 393224 | tf_op jit(solution)/shard_map/ppermute | solution.py:424
  89.9 4.8 %collective-permute-start.8 = (f32[32,1024]{1,0:T(8,128)S(1)}, f32[32,1024]{1,0:T(8,128)S(1)}, u32[]{:S(2)}, u32[]{:S(2)}) collective-permute-start(f32[32,1024]{1,0:T(8,128)S(1)} %get-tuple-element.34), channel_id=1, source_target_pairs={{8,24},{9,25},{10,26},{11,27},{12,28},{13,29},{14,30},{15,31}} | collective-permute-start | bytes 393224 | tf_op jit(solution)/shard_map/ppermute | solution.py:424
  90.6 9.9 %collective-permute-start.5 = (f32[32,1024]{1,0:T(8,128)S(1)}, f32[32,1024]{1,0:T(8,128)S(1)}, u32[]{:S(2)}, u32[]{:S(2)}) collective-permute-start(f32[32,1024]{1,0:T(8,128)S(1)} %get-tuple-element.35), channel_id=1, source_target_pairs={{16,24},{17,25},{18,26},{19,27},{20,28},{21,29},{22,30},{23,31}} | collective-permute-start | bytes 393224 | tf_op jit(solution)/shard_map/ppermute | solution.py:427
  100.5 1.6 %collective-permute-start.9 = (f32[32,1024]{1,0:T(8,128)S(1)}, f32[32,1024]{1,0:T(8,128)S(1)}, u32[]{:S(2)}, u32[]{:S(2)}) collective-permute-start(f32[32,1024]{1,0:T(8,128)S(1)} %get-tuple-element.32), channel_id=1, source_target_pairs={{0,4},{4,0},{1,5},{5,1},{2,6},{6,2},{3,7},{7,3},{8,12},{12,8},{9,1... | collective-permute-start | bytes 393224 | tf_op jit(solution)/shard_map/ppermute | solution.py:521
  102.1 0.7 copy-start.3
where the time goes:
time: 113 us; the launch traced here: 112 us
  waiting for transfers between devices  41.5 us (37%)
  starting transfers between devices  29.7 us (26%)
  Pallas kernels  24.3 us (22%)
  local copies, waits for them, and re-layouts  11.8 us (10%)
  other arithmetic  3.45 us (3%)
    all_to_all x2, waiting for transfers between devices, local(): received = lax.all_to_all(sent, ('core', 'trans'), 0, 0, tiled=True)  25.8 us
    pallas_call x6, Pallas kernels, call(): pl.pallas_call(kernel, out_shape=[jax.ShapeDtypeStruct(shape, kind) for s...  24.3 us
    ppermute x6, starting transfers between devices, entering_chip(): got_gained = got_gained + lax.ppermute(gained, 'z', pairs)  12.1 us
    all_to_all x2, starting transfers between devices, local(): received = lax.all_to_all(sent, ('core', 'trans'), 0, 0, tiled=True)  11.5 us
    unnamed x11, local copies, waits for them, and re-layouts  10.4 us
    ppermute x6, waiting for transfers between devices, entering_chip(): got_gained = got_gained + lax.ppermute(gained, 'z', pairs)  8.11 us
    ppermute x2, waiting for transfers between devices, entering_chip(): got_growth = got_growth + lax.ppermute(growth, 'z', later)  5.72 us
    ppermute x2, starting transfers between devices, entering_chip(): got_growth = got_growth + lax.ppermute(growth, 'z', later)  5.41 us
  transfers between devices with their start and end apart: 12, of which 8 were waited for; matrix products, arithmetic and copies ran while one was open for 3% of the time, Pallas kernels for 2%

commit v1 on v0

v1 whole, which is shorter than its diff:
```python
import functools
import math

import jax
import jax.numpy as jnp
from jax import lax
from jax.experimental import pallas as pl
from jax.experimental.pallas import tpu as pltpu
from jax.sharding import Mesh
from jax.sharding import PartitionSpec as P

PHOTONS = 8
STEPS = 2
RATE_COEF = 1.8e-08
RECOMB = 0.02
KERR_COEF = 0.3
PLASMA = 4.0
LANES = 128
HALF = LANES // 2
VMEM_LIMIT = 16 * 1024 * 1024
F32 = jnp.float32
BF16 = jnp.bfloat16
VMEM_SPEC = pl.BlockSpec(memory_space=pltpu.VMEM)
ANY_SPEC = pl.BlockSpec(memory_space=pl.ANY)
HBM_SPEC = pl.BlockSpec(memory_space=pltpu.MemorySpace.HBM)


def sincos(angle):
    turns = jnp.floor(angle * (2.0 / math.pi) + 0.5)
    rest = angle - turns * 1.5703125
    rest = rest - turns * 4.837512969970703125e-4
    rest = rest - turns * 7.54978995489188e-8
    square = rest * rest
    sine = ((-1.9515295891e-4 * square + 8.3321608736e-3) * square - 1.6666654611e-1) * square
    sine = sine * rest + rest
    cosine = (2.443315711809948e-5 * square - 1.388731625493765e-3) * square
    cosine = (cosine + 4.166664568298827e-2) * (square * square) - 0.5 * square + 1.0
    quadrant = turns.astype(jnp.int32)
    odd = (quadrant & 1) == 1
    sine, cosine = jnp.where(odd, cosine, sine), jnp.where(odd, sine, cosine)
    sine = jnp.where((quadrant & 2) == 2, -sine, sine)
    cosine = jnp.where(((quadrant + 1) & 2) == 2, -cosine, cosine)
    return sine, cosine


def split3(value):
    high = value.astype(BF16)
    rest = value - high.astype(F32)
    middle = rest.astype(BF16)
    low = (rest - middle.astype(F32)).astype(BF16)
    return high, middle, low


def turned(value, order, position, sign):
    re, im = value
    eighth = (position * 8) // order
    if (position * 8) % order == 0 and eighth % 2 == 0:
        quarter = (eighth // 2 * sign) % 4
        return ((re, im), (-im, re), (-re, -im), (im, -re))[quarter]
    angle = sign * 2.0 * math.pi * position / order
    c, s = math.cos(angle), math.sin(angle)
    if (position * 8) % order == 0:
        root = math.sqrt(0.5)
        sc, ss = math.copysign(1, c), math.copysign(1, s)
        one = re - im if sc == ss else re + im
        two = re + im if sc == ss else re - im
        new_re = one * (root * sc)
        new_im = two * (root * ss) if sc == ss else two * (root * ss)
        return (new_re, new_im)
    return (re * c - im * s, re * s + im * c)


def small_dft(values, sign):
    count = len(values)
    if count == 1:
        return values
    even = small_dft(values[0::2], sign)
    odd = small_dft(values[1::2], sign)
    upper, lower = [], []
    for k in range(count // 2):
        other = turned(odd[k], count, k, sign)
        upper.append((even[k][0] + other[0], even[k][1] + other[1]))
        lower.append((even[k][0] - other[0], even[k][1] - other[1]))
    return upper + lower


def ionise(re, im, density):
    intensity = re * re + im * im
    power = intensity * intensity
    power = power * power
    rate = RATE_COEF * (power * power)
    loss = rate + RECOMB
    decay = jnp.exp(-loss)
    source = (1.0 - decay) * density * rate / loss
    return decay, source


def rotate(re, im, electrons):
    intensity = re * re + im * im
    sine, cosine = sincos(KERR_COEF * intensity - PLASMA * electrons)
    return re * cosine - im * sine, re * sine + im * cosine


def wave(shape, order, sign):
    product = lax.broadcasted_iota(jnp.int32, shape, 0) * lax.broadcasted_iota(jnp.int32, shape, 1)
    sine, cosine = sincos((product % order).astype(F32) * (2.0 * math.pi / order))
    return cosine, sign * sine


def toeplitz_blocks(phase, radix, sign):
    length = radix * LANES
    waves = jnp.concatenate(wave((LANES, LANES), length, sign), axis=1)
    block_re, block_im = wave((radix, LANES), radix, sign)
    block_re, block_im = block_re * (1.0 / length), block_im * (1.0 / length)
    sine, cosine = sincos(phase)
    lane = lax.broadcasted_iota(jnp.int32, phase.shape, 1) % radix
    picked = [jnp.where(lane == k, part, 0.0) for part in (cosine, sine) for k in range(radix)]
    spectrum = jnp.dot(
        jnp.concatenate(picked, axis=0),
        waves,
        precision=lax.Precision.HIGHEST,
        preferred_element_type=F32,
    )
    half = radix * radix
    row = lax.broadcasted_iota(jnp.int32, (LANES, LANES), 0)
    column = lax.broadcasted_iota(jnp.int32, (LANES, LANES), 1)
    direct = column >= row
    blocks = []
    for k in range(radix):
        ours = slice(k * radix, (k + 1) * radix)
        theirs = slice(half + k * radix, half + (k + 1) * radix)
        re = spectrum[ours, :LANES] - spectrum[theirs, LANES:]
        im = spectrum[ours, LANES:] + spectrum[theirs, :LANES]
        full_re = jnp.sum(re * block_re - im * block_im, axis=0, keepdims=True)
        full_im = jnp.sum(re * block_im + im * block_re, axis=0, keepdims=True)
        spread_re = jnp.broadcast_to(full_re, (LANES, LANES))
        spread_im = jnp.broadcast_to(full_im, (LANES, LANES))
        rolled = (
            pltpu.roll(spread_re, 0, 1, stride=1, stride_axis=0),
            pltpu.roll(spread_im, 0, 1, stride=1, stride_axis=0),
        )
        wrapped = turned(rolled, radix, k, -sign)
        blocks.append(
            (jnp.where(direct, rolled[0], wrapped[0]), jnp.where(direct, rolled[1], wrapped[1]))
        )
    return blocks


def store_parts(table_ref, blocks):
    for k, (re, im) in enumerate(blocks):
        for part, (a, b) in enumerate(zip(split3(re), split3(im), strict=True)):
            table_ref[k, part, 0] = a
            table_ref[k, part, 1] = b


def table_kernel(sign, phase_ref, *refs):
    table_ref = refs[-1]
    store_parts(table_ref, toeplitz_blocks(phase_ref[...], table_ref.shape[0], sign))


def forward_y(load, start, step, radix, parts_ref):
    blocks = small_dft([load(a) for a in range(radix)], -1)
    for k, (re, im) in enumerate(blocks):
        for part, (a, b) in enumerate(zip(split3(re), split3(im), strict=True)):
            parts_ref[k, part, start : start + step, :LANES] = a
            parts_ref[k, part, start : start + step, LANES:] = b


def product_y(parts_ref, table_ref, out_ref, radix):
    for k in range(radix):
        high, middle, low = parts_ref[k, 0], parts_ref[k, 1], parts_ref[k, 2]
        left = jnp.concatenate([high, high, high, middle, middle, low], axis=1)
        rights = []
        for part in range(3):
            re, im = table_ref[k, part, 0], table_ref[k, part, 1]
            rights.append(jnp.concatenate([re, im], axis=1))
            rights.append(jnp.concatenate([-im, re], axis=1))
        right = jnp.concatenate(rights + rights[:4] + rights[:2], axis=0)
        out_ref[k] = jnp.dot(left, right, preferred_element_type=F32)


def backward_y(out_ref, start, step, radix):
    picked = [
        (out_ref[k, start : start + step, :LANES], out_ref[k, start : start + step, LANES:])
        for k in range(radix)
    ]
    return small_dft(picked, 1)


def upper_lanes(shape):
    return lax.broadcasted_iota(jnp.int32, shape, 1) >= HALF


def swap_halves(value):
    return pltpu.roll(value, HALF, 1)


def first_kernel(
    packed, light_hbm, phase_hbm, send_hbm, table_ref, parts_ref, mid_ref, light_ref, phase_ref, send_ref, sem
):
    radix = table_ref.shape[0]
    _, across, times, _ = light_ref.shape
    width = send_ref.shape[-1]
    step = min(16, across)
    chunks = range(0, across, step)
    phase_copy = pltpu.make_async_copy(phase_hbm, phase_ref, sem.at[0])
    phase_copy.start()
    arriving = []
    for i, x in enumerate(chunks):
        rows = pl.ds(x, step)
        copy = pltpu.make_async_copy(light_hbm.at[:, rows], light_ref.at[:, rows], sem.at[1 + i])
        copy.start()
        arriving.append(copy)
    phase_copy.wait()
    store_parts(table_ref, toeplitz_blocks(phase_ref[...], radix, 1))
    for copy, x in zip(arriving, chunks, strict=True):
        copy.wait()
        for t in range(times):

            def load(a, x=x, t=t):
                lanes = slice(a * LANES, (a + 1) * LANES)
                rows = slice(x, x + step)
                return light_ref[0, rows, t, lanes], light_ref[1, rows, t, lanes]

            forward_y(load, t * across + x, step, radix, parts_ref)
    product_y(parts_ref, table_ref, mid_ref, radix)
    leaving = []
    upper = upper_lanes((8, LANES))
    for i, begin in enumerate(chunks):
        for x in range(begin, begin + step, 8):
            rows = slice(x, x + 8)
            results = [backward_y(mid_ref, t * across + x, 8, radix) for t in range(times)]
            for a in range(radix):
                for c in range(2):
                    values = [results[t][a][c] for t in range(times)]
                    if packed:
                        one, two = values
                        send_ref[2 * a, c, 0, rows, :] = jnp.where(upper, swap_halves(two), one)
                        send_ref[2 * a + 1, c, 0, rows, :] = jnp.where(upper, two, swap_halves(one))
                    elif width >= LANES:
                        slab, offset = a * LANES // width, a * LANES % width
                        for t in range(times):
                            send_ref[slab, c, t, rows, offset : offset + LANES] = values[t]
                    else:
                        for t in range(times):
                            for piece in range(LANES // width):
                                slab = a * LANES // width + piece
                                lanes = slice(piece * width, (piece + 1) * width)
                                send_ref[slab, c, t, rows, :] = values[t][:, lanes]
        rows = pl.ds(begin, step)
        copy = pltpu.make_async_copy(
            send_ref.at[:, :, :, rows], send_hbm.at[:, :, :, rows], sem.at[1 + i]
        )
        copy.start()
        leaving.append(copy)
    for copy in leaving:
        copy.wait()


def put_x(parts_ref, lanes, start, values):
    step = values[0][0].shape[0]
    for k, (re, im) in enumerate(small_dft(values, -1)):
        for part, (a, b) in enumerate(zip(split3(re), split3(im), strict=True)):
            base = part * 2 * LANES
            parts_ref[k, base + start : base + start + step, lanes] = a
            parts_ref[k, base + LANES + start : base + LANES + start + step, lanes] = b


def product_x(parts_ref, table_ref, out_ref, radix):
    for k in range(radix):
        lefts = []
        for part in range(3):
            re, im = table_ref[k, part, 0], table_ref[k, part, 1]
            lefts.append(jnp.concatenate([re, im], axis=0))
            lefts.append(jnp.concatenate([-im, re], axis=0))
        left = jnp.concatenate(lefts + lefts[:4] + lefts[:2], axis=1)
        high = parts_ref[k, : 2 * LANES]
        middle = parts_ref[k, 2 * LANES : 4 * LANES]
        low = parts_ref[k, 4 * LANES :]
        right = jnp.concatenate([high, high, high, middle, middle, low], axis=0)
        out_ref[k] = jnp.dot(left, right, preferred_element_type=F32)


def get_x(out_ref, lanes, start, step, radix):
    picked = [
        (out_ref[k, start : start + step, lanes], out_ref[k, LANES + start : LANES + start + step, lanes])
        for k in range(radix)
    ]
    return small_dft(picked, 1)


def second_kernel(
    packed, recv_ref, table_ref, density_ref, field_ref, growth_ref, gained_ref, last_growth_ref, last_gained_ref,
    parts_ref, mid_ref,
):
    radix = table_ref.shape[0]
    sources, _, times, across, width = recv_ref.shape
    trans = (radix * LANES) // across
    step = min(16, across)
    total = (sources // trans) * times

    def at(c, t, x):
        place, inner = t // times, t % times
        return recv_ref[place * trans + x // across, c, inner, x % across : x % across + step, :]

    for t in range(total):
        lanes = slice(t * width, (t + 1) * width)
        for start in range(0, LANES, step):
            values = [
                (at(0, t, a * LANES + start), at(1, t, a * LANES + start)) for a in range(radix)
            ]
            put_x(parts_ref, lanes, start, values)
    product_x(parts_ref, table_ref, mid_ref, radix)
    upper = upper_lanes((8, LANES))
    for start in range(0, LANES, 8):
        carry = [None] * radix
        for t in range(total):
            lanes = slice(t * width, (t + 1) * width)
            for a, (re, im) in enumerate(get_x(mid_ref, lanes, start, 8, radix)):
                rows = slice(a * LANES + start, a * LANES + start + 8)
                field_ref[0, t, rows, :] = re
                field_ref[1, t, rows, :] = im
                growth, gained = ionise(re, im, density_ref[rows, :])
                if packed:
                    gained = jnp.where(upper, growth * swap_halves(gained) + gained, gained)
                    growth = jnp.where(upper, growth * swap_halves(growth), growth)
                if carry[a] is not None:
                    gained = growth * carry[a][1] + gained
                    growth = growth * carry[a][0]
                growth_ref[t, rows, :] = growth
                gained_ref[t, rows, :] = gained
                if packed:
                    growth = jnp.where(upper, growth, swap_halves(growth))
                    gained = jnp.where(upper, gained, swap_halves(gained))
                carry[a] = (growth, gained)
        for a in range(radix // 2 if packed else radix):
            rows = slice(a * LANES + start, a * LANES + start + 8)
            growth, gained = carry[a]
            if packed:
                growth = jnp.where(upper, carry[a + radix // 2][0], growth)
                gained = jnp.where(upper, carry[a + radix // 2][1], gained)
            last_growth_ref[rows, :] = growth
            last_gained_ref[rows, :] = gained


def third_kernel(
    packed, field_ref, growth_ref, gained_ref, entering_ref, table_ref, send_hbm, token_ref,
    parts_ref, mid_ref, send_ref, sem,
):
    radix = table_ref.shape[0]
    _, total, _, width = field_ref.shape
    slabs, _, times, across, _ = send_ref.shape
    trans = (radix * LANES) // across
    token_ref[...] = jnp.zeros_like(token_ref)
    step = 16
    upper = upper_lanes((step, LANES))
    for start in range(0, LANES, step):
        entering = []
        for a in range(radix):
            if packed:
                base = (a % (radix // 2)) * LANES + start
                value = entering_ref[base : base + step, :]
                other = swap_halves(value)
                first = a < radix // 2
                entering.append(jnp.where(upper, other if first else value, value if first else other))
            else:
                entering.append(entering_ref[a * LANES + start : a * LANES + start + step, :])
        for t in range(total):
            lanes = slice(t * width, (t + 1) * width)
            values = []
            for a in range(radix):
                rows = slice(a * LANES + start, a * LANES + start + step)
                electrons = growth_ref[t, rows, :] * entering[a] + gained_ref[t, rows, :]
                values.append(rotate(field_ref[0, t, rows, :], field_ref[1, t, rows, :], electrons))
            put_x(parts_ref, lanes, start, values)
    product_x(parts_ref, table_ref, mid_ref, radix)
    leaving = []
    for t in range(total):
        lanes = slice(t * width, (t + 1) * width)
        place, inner = t // times, t % times
        for start in range(0, LANES, 8):
            for a, pair in enumerate(get_x(mid_ref, lanes, start, 8, radix)):
                x = a * LANES + start
                row = x % across
                for c in range(2):
                    send_ref[place * trans + x // across, c, inner, row : row + 8, :] = pair[c]
        if inner == times - 1:
            block = pl.ds(place * trans, trans)
            copy = pltpu.make_async_copy(send_ref.at[block], send_hbm.at[block], sem.at[place])
            copy.start()
            leaving.append(copy)
    for copy in leaving:
        copy.wait()


def fourth_kernel(
    packed, recv_ref, table_ref, density_ref, field_ref, growth_ref, gained_ref, mine_ref, theirs_ref,
    parts_ref, mid_ref,
):
    radix = table_ref.shape[0]
    _, times, across, _ = field_ref.shape
    width = recv_ref.shape[-1]
    core = lax.axis_index("core")
    step = min(16, across)
    upper = upper_lanes((step, LANES))

    def part(c, t, x, a):
        rows = slice(x, x + step)
        if packed:
            one, two = recv_ref[2 * a, c, 0, rows, :], recv_ref[2 * a + 1, c, 0, rows, :]
            if t == 0:
                return jnp.where(upper, swap_halves(two), one)
            return jnp.where(upper, two, swap_halves(one))
        if width >= LANES:
            slab, offset = a * LANES // width, a * LANES % width
            return recv_ref[slab, c, t, rows, offset : offset + LANES]
        pieces = LANES // width
        return jnp.concatenate(
            [recv_ref[a * pieces + p, c, t, rows, :] for p in range(pieces)], axis=1
        )

    for x in range(0, across, step):
        for t in range(times):

            def load(a, x=x, t=t):
                return part(0, t, x, a), part(1, t, x, a)

            forward_y(load, t * across + x, step, radix, parts_ref)
    product_y(parts_ref, table_ref, mid_ref, radix)
    half = across // 2
    for x in range(0, across, 8):
        rows = slice(x, x + 8)
        growth, gained = [None] * radix, [None] * radix
        for t in range(times):
            for a, (re, im) in enumerate(backward_y(mid_ref, t * across + x, 8, radix)):
                lanes = slice(a * LANES, (a + 1) * LANES)
                field_ref[0, t, rows, lanes] = re
                field_ref[1, t, rows, lanes] = im
                decay, source = ionise(re, im, density_ref[rows, lanes])
                if t == 0:
                    growth[a], gained[a] = decay, source
                else:
                    gained[a] = decay * gained[a] + source
                    growth[a] = growth[a] * decay
                growth_ref[t, rows, lanes] = growth[a]
                gained_ref[t, rows, lanes] = gained[a]
    last = times - 1

    def hand_out(own):
        kept, given = slice(own * half, (own + 1) * half), slice((1 - own) * half, (2 - own) * half)
        mine_ref[0] = growth_ref[last, kept, :]
        mine_ref[1] = gained_ref[last, kept, :]
        theirs_ref[0] = growth_ref[last, given, :]
        theirs_ref[1] = gained_ref[last, given, :]

    pl.when(core == 0)(functools.partial(hand_out, 0))
    pl.when(core == 1)(functools.partial(hand_out, 1))


def fifth_kernel(
    field_ref, growth_ref, gained_ref, kept_ref, given_ref, light_hbm, electrons_hbm, light_ref, electrons_ref, sem
):
    _, times, across, length = field_ref.shape
    half = across // 2
    core = lax.axis_index("core")
    step = min(16, half)
    leaving = []
    for i, begin in enumerate(range(0, across, step)):
        for x in range(begin, begin + step, 8):
            own, row = x // half, x % half
            rows = slice(x, x + 8)
            entering = jnp.where(core == own, kept_ref[row : row + 8, :], given_ref[row : row + 8, :])
            for t in range(times):
                for a in range(length // LANES):
                    lanes = slice(a * LANES, (a + 1) * LANES)
                    electrons = (
                        growth_ref[t, rows, lanes] * entering[:, lanes] + gained_ref[t, rows, lanes]
                    )
                    re, im = rotate(field_ref[0, t, rows, lanes], field_ref[1, t, rows, lanes], electrons)
                    light_ref[0, rows, t, lanes] = re
                    light_ref[1, rows, t, lanes] = im
                    electrons_ref[rows, t, lanes] = electrons
        block = pl.ds(begin, step)
        for copy in (
            pltpu.make_async_copy(light_ref.at[:, block], light_hbm.at[:, block], sem.at[0, i]),
            pltpu.make_async_copy(electrons_ref.at[block], electrons_hbm.at[block], sem.at[1, i]),
        ):
            copy.start()
            leaving.append(copy)
    for copy in leaving:
        copy.wait()


def call(kernel, operands, outs, scratch=()):
    return pl.pallas_call(
        kernel,
        out_shape=[jax.ShapeDtypeStruct(shape, kind) for shape, kind, _ in outs],
        in_specs=[spec for _, spec in operands],
        out_specs=[spec for _, _, spec in outs],
        scratch_shapes=list(scratch),
        compiler_params=pltpu.CompilerParams(vmem_limit_bytes=VMEM_LIMIT),
    )(*[array for array, _ in operands])


def fuse(function, *arrays):
    outs = jax.eval_shape(function, *arrays)

    def kernel(*refs):
        results = function(*[ref[...] for ref in refs[: len(arrays)]])
        for ref, result in zip(refs[len(arrays) :], results, strict=True):
            ref[...] = result

    return call(
        kernel,
        [(array, VMEM_SPEC) for array in arrays],
        [(out.shape, out.dtype, VMEM_SPEC) for out in outs],
    )


def scan_levels(axis, growth, gained):
    count = lax.axis_size(axis)
    kept = []
    size = 1
    while size < count:
        need_growth = 2 * size < count
        got_gained, got_growth = [], []
        for reach in range(1, size + 1):
            pairs = [
                (b + size - 1, b + size - 1 + reach)
                for b in range(0, count, 2 * size)
                if b + size - 1 + reach < count
            ]
            got_gained.append(lax.ppermute(gained, axis, pairs))
            if need_growth:
                later = [pair for pair in pairs if pair[0] >= 2 * size]
                got_growth.append(lax.ppermute(growth, axis, later))
        kept.append((got_gained, got_growth))
        if need_growth and 4 * size < count:

            def both(growth, gained, *got):
                new_gained, new_growth = sum(got[: len(got) // 2]), sum(got[len(got) // 2 :])
                return growth * new_growth, growth * new_gained + gained

            growth, gained = fuse(both, growth, gained, *got_gained, *got_growth)
        elif need_growth:
            (gained,) = fuse(
                lambda growth, gained, *got: (growth * sum(got) + gained,), growth, gained, *got_gained
            )
        size *= 2
    return kept


def finish_scan(axis, levels):
    place = lax.axis_index(axis)
    before_growth = before_gained = None
    for level, (got_gained, got_growth) in enumerate(levels):
        new_gained = sum(got_gained)
        upper = (place // 2**level) % 2 == 1
        if before_gained is None:
            before_gained = new_gained
        else:
            before_gained = before_growth * new_gained + before_gained
        if got_growth:
            new_growth = sum(got_growth)
            if before_growth is None:
                before_growth = jnp.where(upper, new_growth, 1.0)
            else:
                before_growth = jnp.where(upper, before_growth * new_growth, before_growth)
    return before_gained


def flatten(levels):
    leaves, tree = jax.tree.flatten(levels)
    return leaves, lambda values: jax.tree.unflatten(tree, values)


def local(packed, light_field, gas_density, phase_x, phase_y):
    width_x, width_y = phase_x.shape[0], phase_y.shape[0]
    radix_x, radix_y = width_x // LANES, width_y // LANES
    _, across, times, _ = light_field.shape
    group = ("zl", "core", "trans") if packed else ("core", "trans")
    later = "zh" if packed else ("zh", "zl")
    whole = ("zh", "zl")
    slabs = lax.axis_size(group)
    width = width_y // slabs
    slab = lax.axis_index(group)
    trans = lax.axis_size("trans")
    density_y = lax.dynamic_slice_in_dim(gas_density, slab * width, width, 1)
    density_x = lax.dynamic_slice_in_dim(gas_density, lax.axis_index("trans") * across, across, 0)
    if packed:
        density_y = jnp.concatenate([density_y] * times, axis=1)
        sent_shape = (slabs, 2, 1, across, times * width)
    else:
        sent_shape = (slabs, 2, times, across, width)
    inner, lanes = sent_shape[2], sent_shape[4]
    total = (slabs // trans) * inner
    rows = times * across

    def vmem(*shapes):
        return [(shape, F32, VMEM_SPEC) for shape in shapes]

    scratch_y = [
        pltpu.VMEM((radix_y, 3, rows, 2 * LANES), BF16),
        pltpu.VMEM((radix_y, rows, 2 * LANES), F32),
    ]
    scratch_x = [
        pltpu.VMEM((radix_x, 6 * LANES, total * lanes), BF16),
        pltpu.VMEM((radix_x, 2 * LANES, total * lanes), F32),
    ]
    table_y_shape = (radix_y, 3, 2, LANES, LANES)
    phase_y = phase_y.reshape(radix_y, LANES)
    (table_x,) = call(
        functools.partial(table_kernel, -1),
        [(phase_x.reshape(radix_x, LANES), VMEM_SPEC)],
        [((radix_x, 3, 2, LANES, LANES), BF16, VMEM_SPEC)],
    )
    (sent,) = call(
        functools.partial(first_kernel, packed),
        [(light_field, ANY_SPEC), (phase_y, ANY_SPEC)],
        [(sent_shape, F32, HBM_SPEC)],
        [pltpu.VMEM(table_y_shape, BF16)]
        + scratch_y
        + [
            pltpu.VMEM(light_field.shape, F32),
            pltpu.VMEM(phase_y.shape, F32),
            pltpu.VMEM(sent_shape, F32),
            pltpu.SemaphoreType.DMA((1 + across // min(16, across),)),
        ],
    )
    received = lax.all_to_all(sent, group, 0, 0, tiled=True)
    cells = (width_x, lanes)
    last = (width_x // 2, lanes) if packed else cells
    field, growth, gained, last_growth, last_gained = call(
        functools.partial(second_kernel, packed),
        [(received, VMEM_SPEC), (table_x, VMEM_SPEC), (density_y, VMEM_SPEC)],
        vmem((2, total) + cells, (total,) + cells, (total,) + cells, last, last),
        scratch_x,
    )
    levels = scan_levels(later, last_growth, last_gained)
    if len(levels) == 1 and len(levels[0][0]) == 1:
        entering = levels[0][0][0]
    else:
        leaves, rebuild = flatten(levels)
        (entering,) = fuse(lambda *got: (finish_scan(later, rebuild(got)),), *leaves)
    sent, token = call(
        functools.partial(third_kernel, packed),
        [(array, VMEM_SPEC) for array in (field, growth, gained, entering, table_x)],
        [(sent_shape, F32, HBM_SPEC), ((8, LANES), F32, VMEM_SPEC)],
        scratch_x + [pltpu.VMEM(sent_shape, F32), pltpu.SemaphoreType.DMA((slabs // trans,))],
    )
    received = lax.all_to_all(sent, group, 0, 0, tiled=True)
    (table_y,) = call(
        functools.partial(table_kernel, 1),
        [(phase_y, VMEM_SPEC), (token, VMEM_SPEC)],
        [(table_y_shape, BF16, VMEM_SPEC)],
    )
    cells = (across, width_y)
    half = (2, across // 2, width_y)
    field, growth, gained, mine, theirs = call(
        functools.partial(fourth_kernel, packed),
        [(received, VMEM_SPEC), (table_y, VMEM_SPEC), (density_x, VMEM_SPEC)],
        vmem((2, times) + cells, (times,) + cells, (times,) + cells, half, half),
        scratch_y,
    )
    swap = [(0, 1), (1, 0)]
    other = lax.ppermute(theirs, "core", swap)

    def ordered(mine, other):
        first = lax.axis_index("core") == 0
        early = [jnp.where(first, mine[i], other[i]) for i in range(2)]
        late = [jnp.where(first, other[i], mine[i]) for i in range(2)]
        return early, late

    def chip_map(mine, other):
        early, late = ordered(mine, other)
        return late[0] * early[0], late[0] * early[1] + late[1]

    levels = scan_levels(whole, *fuse(chip_map, mine, other))
    leaves, rebuild = flatten(levels)

    def hand_over(mine, other, *got):
        early, _ = ordered(mine, other)
        first = lax.axis_index("core") == 0
        entering = finish_scan(whole, rebuild(got))
        halfway = early[0] * entering + early[1]
        return jnp.where(first, entering, halfway), jnp.where(first, halfway, entering)

    kept, given = fuse(hand_over, mine, other, *leaves)
    given = lax.ppermute(given, "core", swap)
    chunks = across // min(16, across // 2)
    return call(
        fifth_kernel,
        [(array, VMEM_SPEC) for array in (field, growth, gained, kept, given)],
        [(light_field.shape, F32, HBM_SPEC), ((across, times, width_y), F32, HBM_SPEC)],
        [
            pltpu.VMEM(light_field.shape, F32),
            pltpu.VMEM((across, times, width_y), F32),
            pltpu.SemaphoreType.DMA((2, chunks)),
        ],
    )


def solution(mesh):
    slabs, trans = mesh.shape["tm"], mesh.shape["trans"]

    def run(light_field, gas_density, phase_x, phase_y):
        times = light_field.shape[2] // slabs
        width = phase_y.shape[0] // (trans * 4)
        packed = (
            slabs % 4 == 0
            and slabs > 4
            and times == 2
            and times * width == LANES
            and phase_x.shape[0] % (2 * LANES) == 0
        )
        pair = 2 if packed else 1
        split = Mesh(
            mesh.devices.reshape(slabs // (2 * pair), pair, 2, trans), ("zh", "zl", "core", "trans")
        )
        time_axes = ("zh", "zl", "core")
        placed = (P(None, "trans", time_axes, None), P(), P(), P())
        return jax.shard_map(
            functools.partial(local, packed),
            mesh=split,
            in_specs=placed,
            out_specs=(P(None, "trans", time_axes, None), P("trans", time_axes, None)),
            check_vma=False,
        )(light_field, gas_density, phase_x, phase_y)

    return run
```

time: 113 us -> 90.3 us (0.80)
  local copies, waits for them, and re-layouts: 11.8 us -> 2.14 us
  starting transfers between devices: 29.7 us -> 20.9 us
  other arithmetic: 3.45 us -> 0.1 us
  Pallas kernels: 24.3 us -> 21.3 us
  waiting for transfers between devices: 41.5 us -> 44.4 us
    unnamed x11 -> x10, local copies, waits for them, and re-layouts: 10.4 us -> 2.01 us
    ppermute x9 -> x6, starting transfers between devices: 18.1 us -> 9.83 us  [the longest x4 5.6 us: scan_levels(): got_gained.append(lax.ppermute(gained, axis, pairs))]
    select_n x6 -> x0, other arithmetic: 3.42 us -> none  [the longest x2 1.02 us: entering_chip(): jnp.where(upper, growth * got_gained + gained, gained)]
    pallas_call x6 -> x10, Pallas kernels: 24.3 us -> 21.3 us  [call(): pl.pallas_call(kernel, out_shape=[jax.ShapeDtypeStruct(shape, kind) for s...]
    all_to_all x2, waiting for transfers between devices: 25.8 us -> 28.3 us  [local(): received = lax.all_to_all(sent, group, 0, 0, tiled=True)]
    ppermute x9 -> x6, waiting for transfers between devices: 14.1 us -> 14.8 us  [the longest x4 13 us: scan_levels(): got_gained.append(lax.ppermute(gained, axis, pairs))]
  transfers between devices with their start and end apart: 12 -> 9, of which waited for: 8 -> 8; matrix products, arithmetic and copies ran while one was open for 3% -> 0% of each run, Pallas kernels for 2% -> 1%
where the time goes in v1:
time: 90.3 us; the launch traced here: 89.8 us
  waiting for transfers between devices  44.4 us (49%)
  Pallas kernels  21.3 us (24%)
  starting transfers between devices  20.9 us (23%)
  local copies, waits for them, and re-layouts  2.14 us (2%)
  between operations  0.96 us (1%)
    all_to_all x2, waiting for transfers between devices, local(): received = lax.all_to_all(sent, group, 0, 0, tiled=True)  28.3 us
    pallas_call x10, Pallas kernels, call(): pl.pallas_call(kernel, out_shape=[jax.ShapeDtypeStruct(shape, kind) for s...  21.3 us
    ppermute x4, waiting for transfers between devices, scan_levels(): got_gained.append(lax.ppermute(gained, axis, pairs))  13 us
    all_to_all x2, starting transfers between devices, local(): received = lax.all_to_all(sent, group, 0, 0, tiled=True)  10.8 us
    ppermute x4, starting transfers between devices, scan_levels(): got_gained.append(lax.ppermute(gained, axis, pairs))  5.6 us
    ppermute x1, starting transfers between devices, local(): given = lax.ppermute(given, 'core', swap)  2.93 us
    unnamed x10, local copies, waits for them, and re-layouts  2.01 us
  transfers between devices with their start and end apart: 9, of which 8 were waited for; matrix products, arithmetic and copies ran while one was open for 0% of the time, Pallas kernels for 1%

profile of v1, /device:TPU:17, one launch (start us, length us, event | category | flops | bytes accessed | tf_op | source)
XLA Modules:
  0.0 89.8 jit_solution(6682611109348740165)
XLA Ops:
  0.6 0.0 copy-start
  0.6 0.0 copy-start.1
  0.7 1.3 %copy-done.1 = f32[2,64,2,1024]{3,2,1,0:T(2,128)S(1)} copy-done((f32[2,64,2,1024]{3,2,1,0:T(2,128)S(1)}, f32[2,64,2,1024]{3,2,1,0:T(2,128)}, u32[]{:S(2)}) %copy-start.1) | copy-done | bytes 1048600
  2.0 0.0 copy-start.2
  2.0 0.7 copy-done.2
  2.6 8.8 %shard_map.59 = f32[16,2,1,64,128]{4,3,2,1,0:T(8,128)} custom-call(f32[2,64,2,1024]{3,2,1,0:T(2,128)S(1)} %copy-done.1, f32[8,128]{1,0:T(8,128)S(1)} %bitcast.2), custom_call_target="tpu_custom_call" | custom-call | tf_op jit(solution)/shard_map/pallas_call | solution.py:495
  11.4 0.0 copy-start.4
  11.4 5.4 %all-to-all-start = ((f32[16,2,1,64,128]{4,3,2,1,0:T(8,128)}), f32[16,2,1,64,128]{4,3,2,1,0:T(8,128)S(1)}, u32[]{:S(2)}, u32[]{:S(2)}) async-start(f32[16,2,1,64,128]{4,3,2,1,0:T(8,128)} %shard_map.59), calls=%async_computation | async-start | bytes 2097152 | tf_op jit(solution)/shard_map/all_to_all | solution.py:630
  16.9 0.0 copy-done.4
  16.9 0.4 shard_map.60.table_ref
  17.3 0.0 copy-done
  17.3 0.1 constant_dynamic-slice_fusion.1
  17.4 0.1 pad_maximum_fusion.density_ref
  17.5 14.2 %all-to-all-done.recv_ref = f32[16,2,1,64,128]{4,3,2,1,0:T(8,128)S(1)} async-done(((f32[16,2,1,64,128]{4,3,2,1,0:T(8,128)}), f32[16,2,1,64,128]{4,3,2,1,0:T(8,128)S(1)}, u32[]{:S(2)}, u32[]{:S(2)}) %all-to-all-start) | async-done | bytes 1048608 | tf_op jit(solution)/shard_map/all_to_all | solution.py:630
  31.7 2.5 %shard_map.61 = (f32[2,4,256,128]{3,2,1,0:T(8,128)S(1)}, f32[4,256,128]{2,1,0:T(8,128)S(1)}, f32[4,256,128]{2,1,0:T(8,128)S(1)}, f32[128,128]{1,0:T(8,128)}, f32[128,128]{1,0:T(8,128)S(1)}) custom-call(f32[16,2,1,64,128]{4,3,2,1,0:T(8,128)S(1)} %all-to-all-done.recv_ref, bf16[2,3,2,128,128]{4,3,2,1,0:T(8,128)(2,1)S(1)} %shard_map.60.table_ref, ...), custom_call_target="tpu_custom_call" | custom-call | tf_op jit(solution)/shard_map/pallas_call | solution.py:495
  34.2 1.5 %collective-permute-start = (f32[128,128]{1,0:T(8,128)S(1)}, f32[128,128]{1,0:T(8,128)S(1)}, u32[]{:S(2)}, u32[]{:S(2)}) collective-permute-start(f32[128,128]{1,0:T(8,128)S(1)} %get-tuple-element.20), channel_id=1, source_target_pairs={{0,16},{1,17},{2,18},{3,19},{4,20},{5,21},{6,22},{7,23},{8,24},{9,... | collective-permute-start | bytes 196616 | tf_op jit(solution)/shard_map/ppermute | solution.py:533
  35.7 4.8 %collective-permute-done.entering_ref = f32[128,128]{1,0:T(8,128)S(1)} collective-permute-done((f32[128,128]{1,0:T(8,128)S(1)}, f32[128,128]{1,0:T(8,128)S(1)}, u32[]{:S(2)}, u32[]{:S(2)}) %collective-permute-start) | collective-permute-done | bytes 65568 | tf_op jit(solution)/shard_map/ppermute | solution.py:533
  40.5 3.2 %shard_map.62 = (f32[16,2,1,64,128]{4,3,2,1,0:T(8,128)}, f32[8,128]{1,0:T(8,128)S(1)}) custom-call(f32[2,4,256,128]{3,2,1,0:T(8,128)S(1)} %get-tuple-element.17.field_ref, f32[4,256,128]{2,1,0:T(8,128)S(1)} %get-tuple-element.18.growth_ref, f32[4,256,128]{2,1,0:T(8,128)S(1)} %get-tuple-element.19.gained_ref, ...), custom_call_target="tpu_custom_call" | custom-call | tf_op jit(solution)/shard_map/pallas_call | solution.py:495
  43.7 0.0 copy-start.3
  43.7 5.4 %all-to-all-start.1 = ((f32[16,2,1,64,128]{4,3,2,1,0:T(8,128)}), f32[16,2,1,64,128]{4,3,2,1,0:T(8,128)}, u32[]{:S(2)}, u32[]{:S(2)}) async-start(f32[16,2,1,64,128]{4,3,2,1,0:T(8,128)} %get-tuple-element.21), calls=%async_computation.1 | async-start | bytes 2097152 | tf_op jit(solution)/shard_map/all_to_all | solution.py:651
  49.1 0.0 copy-done.3
  49.1 0.7 shard_map.63.table_ref
  49.9 14.2 %all-to-all-done.1.recv_ref = f32[16,2,1,64,128]{4,3,2,1,0:T(8,128)} async-done(((f32[16,2,1,64,128]{4,3,2,1,0:T(8,128)}), f32[16,2,1,64,128]{4,3,2,1,0:T(8,128)}, u32[]{:S(2)}, u32[]{:S(2)}) %all-to-all-start.1) | async-done | bytes 1048608 | tf_op jit(solution)/shard_map/all_to_all | solution.py:651
  64.1 2.9 %shard_map.64 = (f32[2,2,64,1024]{3,2,1,0:T(8,128)S(1)}, f32[2,64,1024]{2,1,0:T(8,128)S(1)}, f32[2,64,1024]{2,1,0:T(8,128)S(1)}, f32[2,32,1024]{2,1,0:T(8,128)S(1)}, f32[2,32,1024]{2,1,0:T(8,128)S(1)}) custom-call(f32[16,2,1,64,128]{4,3,2,1,0:T(8,128)} %all-to-all-done.1.recv_ref, bf16[8,3,2,128,128]{4,3,2,1,0:T(8,128)(2,1)S(1)} %shard_map.63.table_ref, ...), custom_call_target="tpu_custom_call" | custom-call | tf_op jit(solution)/shard_map/pallas_call | solution.py:495
  67.0 0.3 collective-permute-start.1
  67.3 1.3 %collective-permute-done.1.refs_1_ = f32[2,32,1024]{2,1,0:T(8,128)S(1)} collective-permute-done((f32[2,32,1024]{2,1,0:T(8,128)S(1)}, f32[2,32,1024]{2,1,0:T(8,128)S(1)}, u32[]{:S(2)}, u32[]{:S(2)}) %collective-permute-start.1) | collective-permute-done | bytes 262176 | tf_op jit(solution)/shard_map/ppermute | solution.py:666
  68.6 2.2 %collective-permute-start.2 = (f32[32,1024]{1,0:T(8,128)S(1)}, f32[32,1024]{1,0:T(8,128)S(1)}, u32[]{:S(2)}, u32[]{:S(2)}) collective-permute-start(f32[32,1024]{1,0:T(8,128)S(1)} %get-tuple-element.28.refs_1_), channel_id=1, source_target_pairs={{0,8},{16,24},{1,9},{17,25},{2,10},{18,26},{3,11},{19,27},{4,12},{... | collective-permute-start | bytes 393224 | tf_op jit(solution)/shard_map/ppermute | solution.py:533
  70.8 1.3 %collective-permute-start.3 = (f32[32,1024]{1,0:T(8,128)S(1)}, f32[32,1024]{1,0:T(8,128)S(1)}, u32[]{:S(2)}, u32[]{:S(2)}) collective-permute-start(f32[32,1024]{1,0:T(8,128)S(1)} %get-tuple-element.29.refs_0_), channel_id=1, source_target_pairs={{16,24},{17,25},{18,26},{19,27},{20,28},{21,29},{22,30},{23,31}} | collective-permute-start | bytes 393224 | tf_op jit(solution)/shard_map/ppermute | solution.py:536
  72.1 1.3 %collective-permute-done.2.refs_2_ = f32[32,1024]{1,0:T(8,128)S(1)} collective-permute-done((f32[32,1024]{1,0:T(8,128)S(1)}, f32[32,1024]{1,0:T(8,128)S(1)}, u32[]{:S(2)}, u32[]{:S(2)}) %collective-permute-start.2) | collective-permute-done | bytes 131104 | tf_op jit(solution)/shard_map/ppermute | solution.py:533
  73.5 0.7 collective-permute-start.5
  74.2 1.3 %collective-permute-start.4 = (f32[32,1024]{1,0:T(8,128)S(1)}, f32[32,1024]{1,0:T(8,128)S(1)}, u32[]{:S(2)}, u32[]{:S(2)}) collective-permute-start(f32[32,1024]{1,0:T(8,128)S(1)} %shard_map.66), channel_id=1, source_target_pairs={{8,16},{9,17},{10,18},{11,19},{12,20},{13,21},{14,22},{15,23}} | collective-permute-start | bytes 393224 | tf_op jit(solution)/shard_map/ppermute | solution.py:533
  75.5 0.8 collective-permute-done.3.refs_3_
  76.3 0.0 collective-permute-done.5.refs_5_
  76.3 6.9 %collective-permute-done.4.refs_4_ = f32[32,1024]{1,0:T(8,128)S(1)} collective-permute-done((f32[32,1024]{1,0:T(8,128)S(1)}, f32[32,1024]{1,0:T(8,128)S(1)}, u32[]{:S(2)}, u32[]{:S(2)}) %collective-permute-start.4) | collective-permute-done | bytes 131104 | tf_op jit(solution)/shard_map/ppermute | solution.py:533
  83.1 0.1 shard_map.67
  83.2 2.9 %collective-permute-start.6 = (f32[32,1024]{1,0:T(8,128)S(1)}, f32[32,1024]{1,0:T(8,128)S(1)}, u32[]{:S(2)}, u32[]{:S(2)}) collective-permute-start(f32[32,1024]{1,0:T(8,128)S(1)} %get-tuple-element.31), channel_id=1, source_target_pairs={{0,4},{4,0},{1,5},{5,1},{2,6},{6,2},{3,7},{7,3},{8,12},{12,8},{9,1... | collective-permute-start | bytes 393224 | tf_op jit(solution)/shard_map/ppermute | solution.py:689
  86.2 1.0 %collective-permute-done.6.given_ref = f32[32,1024]{1,0:T(8,128)S(1)} collective-permute-done((f32[32,1024]{1,0:T(8,128)S(1)}, f32[32,1024]{1,0:T(8,128)S(1)}, u32[]{:S(2)}, u32[]{:S(2)}) %collective-permute-start.6) | collective-permute-done | bytes 131104 | tf_op jit(solution)/shard_map/ppermute | solution.py:689
  87.1 2.5 %shard_map.68 = (f32[2,64,2,1024]{3,2,1,0:T(2,128)}, f32[64,2,1024]{2,1,0:T(2,128)}) custom-call(f32[2,2,64,1024]{3,2,1,0:T(8,128)S(1)} %get-tuple-element.23.field_ref, f32[2,64,1024]{2,1,0:T(8,128)S(1)} %get-tuple-element.24.growth_ref, f32[2,64,1024]{2,1,0:T(8,128)S(1)} %get-tuple-element.25.gained_ref, f32[32,1024]{1,0:T(8,128)S(1)} %get-tuple-element.30.kept_ref, ...), custom_call_target="tpu_custom_call" | custom-call | tf_op jit(solution)/shard_map/pallas_call | solution.py:495
  (3 shorter events, 0.1 us)
Async XLA Ops:
  0.6 16.7 %copy-start = (f32[256,1024]{1,0:T(8,128)S(1)}, f32[256,1024]{1,0:T(8,128)}, u32[]{:S(2)}) copy-start(f32[256,1024]{1,0:T(8,128)} %param.5) | copy-start | bytes 3145732
  0.6 1.3 %copy-start.1 = (f32[2,64,2,1024]{3,2,1,0:T(2,128)S(1)}, f32[2,64,2,1024]{3,2,1,0:T(2,128)}, u32[]{:S(2)}) copy-start(f32[2,64,2,1024]{3,2,1,0:T(2,128)} %light_hbm.1) | copy-start | bytes 3145732
  2.0 0.7 copy-start.2
  11.4 5.5 %copy-start.4 = (f32[256]{0:T(256)S(1)}, f32[256]{0:T(256)}, u32[]{:S(2)}) copy-start(f32[256]{0:T(256)} %param.6) | copy-start | bytes 3076
  11.4 20.3 %all-to-all-start = ((f32[16,2,1,64,128]{4,3,2,1,0:T(8,128)}), f32[16,2,1,64,128]{4,3,2,1,0:T(8,128)S(1)}, u32[]{:S(2)}, u32[]{:S(2)}) async-start(f32[16,2,1,64,128]{4,3,2,1,0:T(8,128)} %shard_map.59), calls=%async_computation | async-start | bytes 2097152 | tf_op jit(solution)/shard_map/all_to_all | solution.py:630
  34.2 6.2 %collective-permute-start = (f32[128,128]{1,0:T(8,128)S(1)}, f32[128,128]{1,0:T(8,128)S(1)}, u32[]{:S(2)}, u32[]{:S(2)}) collective-permute-start(f32[128,128]{1,0:T(8,128)S(1)} %get-tuple-element.20), channel_id=1, source_target_pairs={{0,16},{1,17},{2,18},{3,19},{4,20},{5,21},{6,22},{7,23},{8,24},{9,... | collective-permute-start | bytes 196616 | tf_op jit(solution)/shard_map/ppermute | solution.py:533
  43.7 5.4 %copy-start.3 = (f32[1024]{0:T(1024)S(1)}, f32[1024]{0:T(1024)}, u32[]{:S(2)}) copy-start(f32[1024]{0:T(1024)} %param.7) | copy-start | bytes 12292
  43.7 20.3 %all-to-all-start.1 = ((f32[16,2,1,64,128]{4,3,2,1,0:T(8,128)}), f32[16,2,1,64,128]{4,3,2,1,0:T(8,128)}, u32[]{:S(2)}, u32[]{:S(2)}) async-start(f32[16,2,1,64,128]{4,3,2,1,0:T(8,128)} %get-tuple-element.21), calls=%async_computation.1 | async-start | bytes 2097152 | tf_op jit(solution)/shard_map/all_to_all | solution.py:651
  67.0 1.6 %collective-permute-start.1 = (f32[2,32,1024]{2,1,0:T(8,128)S(1)}, f32[2,32,1024]{2,1,0:T(8,128)S(1)}, u32[]{:S(2)}, u32[]{:S(2)}) collective-permute-start(f32[2,32,1024]{2,1,0:T(8,128)S(1)} %get-tuple-element.27), channel_id=1, source_target_pairs={{0,4},{4,0},{1,5},{5,1},{2,6},{6,2},{3,7},{7,3},{8,12},{12,8},{9,1... | collective-permute-start | bytes 786440 | tf_op jit(solution)/shard_map/ppermute | solution.py:666
  68.6 4.8 %collective-permute-start.2 = (f32[32,1024]{1,0:T(8,128)S(1)}, f32[32,1024]{1,0:T(8,128)S(1)}, u32[]{:S(2)}, u32[]{:S(2)}) collective-permute-start(f32[32,1024]{1,0:T(8,128)S(1)} %get-tuple-element.28.refs_1_), channel_id=1, source_target_pairs={{0,8},{16,24},{1,9},{17,25},{2,10},{18,26},{3,11},{19,27},{4,12},{... | collective-permute-start | bytes 393224 | tf_op jit(solution)/shard_map/ppermute | solution.py:533
  70.8 5.4 %collective-permute-start.3 = (f32[32,1024]{1,0:T(8,128)S(1)}, f32[32,1024]{1,0:T(8,128)S(1)}, u32[]{:S(2)}, u32[]{:S(2)}) collective-permute-start(f32[32,1024]{1,0:T(8,128)S(1)} %get-tuple-element.29.refs_0_), channel_id=1, source_target_pairs={{16,24},{17,25},{18,26},{19,27},{20,28},{21,29},{22,30},{23,31}} | collective-permute-start | bytes 393224 | tf_op jit(solution)/shard_map/ppermute | solution.py:536
  73.5 2.8 %collective-permute-start.5 = (f32[32,1024]{1,0:T(8,128)S(1)}, f32[32,1024]{1,0:T(8,128)S(1)}, u32[]{:S(2)}, u32[]{:S(2)}) collective-permute-start(f32[32,1024]{1,0:T(8,128)S(1)} %shard_map.66), channel_id=1, source_target_pairs={{8,24},{9,25},{10,26},{11,27},{12,28},{13,29},{14,30},{15,31}} | collective-permute-start | bytes 393224 | tf_op jit(solution)/shard_map/ppermute | solution.py:533
  74.2 9.0 %collective-permute-start.4 = (f32[32,1024]{1,0:T(8,128)S(1)}, f32[32,1024]{1,0:T(8,128)S(1)}, u32[]{:S(2)}, u32[]{:S(2)}) collective-permute-start(f32[32,1024]{1,0:T(8,128)S(1)} %shard_map.66), channel_id=1, source_target_pairs={{8,16},{9,17},{10,18},{11,19},{12,20},{13,21},{14,22},{15,23}} | collective-permute-start | bytes 393224 | tf_op jit(solution)/shard_map/ppermute | solution.py:533
  83.2 3.9 %collective-permute-start.6 = (f32[32,1024]{1,0:T(8,128)S(1)}, f32[32,1024]{1,0:T(8,128)S(1)}, u32[]{:S(2)}, u32[]{:S(2)}) collective-permute-start(f32[32,1024]{1,0:T(8,128)S(1)} %get-tuple-element.31), channel_id=1, source_target_pairs={{0,4},{4,0},{1,5},{5,1},{2,6},{6,2},{3,7},{7,3},{8,12},{12,8},{9,1... | collective-permute-start | bytes 393224 | tf_op jit(solution)/shard_map/ppermute | solution.py:689

commit v2 on v1

--- a/solution.py
+++ b/solution.py
@@ -17,6 +17,8 @@
 PLASMA = 4.0
 LANES = 128
 HALF = LANES // 2
+GROUP = {True: ("zl", "core", "trans"), False: ("core", "trans")}
+LATER = {True: ("zh",), False: ("zh", "zl")}
 VMEM_LIMIT = 16 * 1024 * 1024
 F32 = jnp.float32
 BF16 = jnp.bfloat16
@@ -25,9 +27,9 @@
 HBM_SPEC = pl.BlockSpec(memory_space=pltpu.MemorySpace.HBM)
 
 
-def sincos(angle):
-    turns = jnp.floor(angle * (2.0 / math.pi) + 0.5)
-    rest = angle - turns * 1.5703125
+def sincos(quarter):
+    turns = jnp.floor(quarter * (2.0 / math.pi) + 0.5)
+    rest = quarter - turns * 1.5703125
     rest = rest - turns * 4.837512969970703125e-4
     rest = rest - turns * 7.54978995489188e-8
     square = rest * rest
@@ -35,11 +37,9 @@
     sine = sine * rest + rest
     cosine = (2.443315711809948e-5 * square - 1.388731625493765e-3) * square
     cosine = (cosine + 4.166664568298827e-2) * (square * square) - 0.5 * square + 1.0
-    quadrant = turns.astype(jnp.int32)
-    odd = (quadrant & 1) == 1
-    sine, cosine = jnp.where(odd, cosine, sine), jnp.where(odd, sine, cosine)
-    sine = jnp.where((quadrant & 2) == 2, -sine, sine)
-    cosine = jnp.where(((quadrant + 1) & 2) == 2, -cosine, cosine)
+    for _ in range(2):
+        twice = sine + sine
+        sine, cosine = twice * cosine, 1.0 - twice * sine
     return sine, cosine
 
 
@@ -97,13 +97,13 @@
 
 def rotate(re, im, electrons):
     intensity = re * re + im * im
-    sine, cosine = sincos(KERR_COEF * intensity - PLASMA * electrons)
+    sine, cosine = sincos((0.25 * KERR_COEF) * intensity - (0.25 * PLASMA) * electrons)
     return re * cosine - im * sine, re * sine + im * cosine
 
 
 def wave(shape, order, sign):
     product = lax.broadcasted_iota(jnp.int32, shape, 0) * lax.broadcasted_iota(jnp.int32, shape, 1)
-    sine, cosine = sincos((product % order).astype(F32) * (2.0 * math.pi / order))
+    sine, cosine = sincos((product % order).astype(F32) * (0.5 * math.pi / order))
     return cosine, sign * sine
 
 
@@ -112,7 +112,7 @@
     waves = jnp.concatenate(wave((LANES, LANES), length, sign), axis=1)
     block_re, block_im = wave((radix, LANES), radix, sign)
     block_re, block_im = block_re * (1.0 / length), block_im * (1.0 / length)
-    sine, cosine = sincos(phase)
+    sine, cosine = sincos(0.25 * phase)
     lane = lax.broadcasted_iota(jnp.int32, phase.shape, 1) % radix
     picked = [jnp.where(lane == k, part, 0.0) for part in (cosine, sine) for k in range(radix)]
     spectrum = jnp.dot(
@@ -196,7 +196,8 @@
 
 
 def first_kernel(
-    packed, light_hbm, phase_hbm, send_hbm, table_ref, parts_ref, mid_ref, light_ref, phase_ref, send_ref, sem
+    packed, light_hbm, phase_hbm, send_hbm, table_ref, parts_ref, mid_ref, light_ref, rows_ref, phase_ref,
+    send_ref, sem,
 ):
     radix = table_ref.shape[0]
     _, across, times, _ = light_ref.shape
@@ -217,10 +218,14 @@
         copy.wait()
         for t in range(times):
 
+            for c in range(2):
+                for start in range(x, x + step, 8):
+                    rows_ref[c, t, start : start + 8, :] = light_ref[c, start : start + 8, t, :]
+
             def load(a, x=x, t=t):
                 lanes = slice(a * LANES, (a + 1) * LANES)
                 rows = slice(x, x + step)
-                return light_ref[0, rows, t, lanes], light_ref[1, rows, t, lanes]
+                return rows_ref[0, t, rows, lanes], rows_ref[1, t, rows, lanes]
 
             forward_y(load, t * across + x, step, radix, parts_ref)
     product_y(parts_ref, table_ref, mid_ref, radix)
@@ -343,10 +348,14 @@
             last_gained_ref[rows, :] = gained
 
 
-def third_kernel(
-    packed, field_ref, growth_ref, gained_ref, entering_ref, table_ref, send_hbm, token_ref,
-    parts_ref, mid_ref, send_ref, sem,
-):
+def third_kernel(packed, rebuild, leaves, field_ref, growth_ref, gained_ref, table_ref, *refs):
+    got_refs = refs[:leaves]
+    send_hbm, token_ref, parts_ref, mid_ref, send_ref, sem = refs[leaves:]
+
+    def enter(start, step):
+        got = [ref[start : start + step, :] for ref in got_refs]
+        return finish_scan(LATER[packed], rebuild(got))
+
     radix = table_ref.shape[0]
     _, total, _, width = field_ref.shape
     slabs, _, times, across, _ = send_ref.shape
@@ -359,12 +368,12 @@
         for a in range(radix):
             if packed:
                 base = (a % (radix // 2)) * LANES + start
-                value = entering_ref[base : base + step, :]
+                value = enter(base, step)
                 other = swap_halves(value)
                 first = a < radix // 2
                 entering.append(jnp.where(upper, other if first else value, value if first else other))
             else:
-                entering.append(entering_ref[a * LANES + start : a * LANES + start + step, :])
+                entering.append(enter(a * LANES + start, step))
         for t in range(total):
             lanes = slice(t * width, (t + 1) * width)
             values = []
@@ -471,15 +480,18 @@
             rows = slice(x, x + 8)
             entering = jnp.where(core == own, kept_ref[row : row + 8, :], given_ref[row : row + 8, :])
             for t in range(times):
+                results = []
                 for a in range(length // LANES):
                     lanes = slice(a * LANES, (a + 1) * LANES)
                     electrons = (
                         growth_ref[t, rows, lanes] * entering[:, lanes] + gained_ref[t, rows, lanes]
                     )
                     re, im = rotate(field_ref[0, t, rows, lanes], field_ref[1, t, rows, lanes], electrons)
-                    light_ref[0, rows, t, lanes] = re
-                    light_ref[1, rows, t, lanes] = im
-                    electrons_ref[rows, t, lanes] = electrons
+                    results.append((re, im, electrons))
+                re, im, electrons = (jnp.concatenate(part, axis=1) for part in zip(*results, strict=True))
+                light_ref[0, rows, t, :] = re
+                light_ref[1, rows, t, :] = im
+                electrons_ref[rows, t, :] = electrons
         block = pl.ds(begin, step)
         for copy in (
             pltpu.make_async_copy(light_ref.at[:, block], light_hbm.at[:, block], sem.at[0, i]),
@@ -502,6 +514,10 @@
     )(*[array for array, _ in operands])
 
 
+def in_hbm(array):
+    return pltpu.with_memory_space_constraint(array, pltpu.MemorySpace.HBM)
+
+
 def fuse(function, *arrays):
     outs = jax.eval_shape(function, *arrays)
 
@@ -515,6 +531,10 @@
         [(array, VMEM_SPEC) for array in arrays],
         [(out.shape, out.dtype, VMEM_SPEC) for out in outs],
     )
+
+
+def both_ways(pairs):
+    return pairs + [(b, a) for a, b in pairs]
 
 
 def scan_levels(axis, growth, gained):
@@ -530,10 +550,10 @@
                 for b in range(0, count, 2 * size)
                 if b + size - 1 + reach < count
             ]
-            got_gained.append(lax.ppermute(gained, axis, pairs))
+            got_gained.append(lax.ppermute(gained, axis, both_ways(pairs)))
             if need_growth:
                 later = [pair for pair in pairs if pair[0] >= 2 * size]
-                got_growth.append(lax.ppermute(growth, axis, later))
+                got_growth.append(lax.ppermute(growth, axis, both_ways(later)))
         kept.append((got_gained, got_growth))
         if need_growth and 4 * size < count:
 
@@ -557,9 +577,10 @@
         new_gained = sum(got_gained)
         upper = (place // 2**level) % 2 == 1
         if before_gained is None:
-            before_gained = new_gained
+            before_gained = jnp.where(upper, new_gained, 0.0)
         else:
-            before_gained = before_growth * new_gained + before_gained
+            new_gained = before_growth * new_gained + before_gained
+            before_gained = jnp.where(upper, new_gained, before_gained)
         if got_growth:
             new_growth = sum(got_growth)
             if before_growth is None:
@@ -578,8 +599,8 @@
     width_x, width_y = phase_x.shape[0], phase_y.shape[0]
     radix_x, radix_y = width_x // LANES, width_y // LANES
     _, across, times, _ = light_field.shape
-    group = ("zl", "core", "trans") if packed else ("core", "trans")
-    later = "zh" if packed else ("zh", "zl")
+    group = GROUP[packed]
+    later = LATER[packed]
     whole = ("zh", "zl")
     slabs = lax.axis_size(group)
     width = width_y // slabs
@@ -587,6 +608,7 @@
     trans = lax.axis_size("trans")
     density_y = lax.dynamic_slice_in_dim(gas_density, slab * width, width, 1)
     density_x = lax.dynamic_slice_in_dim(gas_density, lax.axis_index("trans") * across, across, 0)
+    density_y, density_x = lax.optimization_barrier((density_y, density_x))
     if packed:
         density_y = jnp.concatenate([density_y] * times, axis=1)
         sent_shape = (slabs, 2, 1, across, times * width)
@@ -616,12 +638,13 @@
     )
     (sent,) = call(
         functools.partial(first_kernel, packed),
-        [(light_field, ANY_SPEC), (phase_y, ANY_SPEC)],
+        [(in_hbm(light_field), HBM_SPEC), (in_hbm(phase_y), HBM_SPEC)],
         [(sent_shape, F32, HBM_SPEC)],
         [pltpu.VMEM(table_y_shape, BF16)]
         + scratch_y
         + [
             pltpu.VMEM(light_field.shape, F32),
+            pltpu.VMEM((2, times, across, width_y), F32),
             pltpu.VMEM(phase_y.shape, F32),
             pltpu.VMEM(sent_shape, F32),
             pltpu.SemaphoreType.DMA((1 + across // min(16, across),)),
@@ -637,14 +660,10 @@
         scratch_x,
     )
     levels = scan_levels(later, last_growth, last_gained)
-    if len(levels) == 1 and len(levels[0][0]) == 1:
-        entering = levels[0][0][0]
-    else:
-        leaves, rebuild = flatten(levels)
-        (entering,) = fuse(lambda *got: (finish_scan(later, rebuild(got)),), *leaves)
+    leaves, rebuild = flatten(levels)
     sent, token = call(
-        functools.partial(third_kernel, packed),
-        [(array, VMEM_SPEC) for array in (field, growth, gained, entering, table_x)],
+        functools.partial(third_kernel, packed, rebuild, len(leaves)),
+        [(array, VMEM_SPEC) for array in (field, growth, gained, table_x, *leaves)],
         [(sent_shape, F32, HBM_SPEC), ((8, LANES), F32, VMEM_SPEC)],
         scratch_x + [pltpu.VMEM(sent_shape, F32), pltpu.SemaphoreType.DMA((slabs // trans,))],
     )

time: 90.3 us -> 80.6 us (0.89)
  the two profiles are of different devices: /device:TPU:17 before, /device:TPU:13 now
where the time goes in v2:
time: 80.6 us; the launch traced here: 80.2 us
  waiting for transfers between devices  40.3 us (50%)
  starting transfers between devices  22.8 us (28%)
  Pallas kernels  16.1 us (20%)
    all_to_all x2, waiting for transfers between devices, local(): received = lax.all_to_all(sent, group, 0, 0, tiled=True)  26 us
    pallas_call x10, Pallas kernels, call(): pl.pallas_call(kernel, out_shape=[jax.ShapeDtypeStruct(shape, kind) for s...  16.1 us
    ppermute x4, waiting for transfers between devices, scan_levels(): got_gained.append(lax.ppermute(gained, axis, both_ways(pairs)))  12.2 us
    all_to_all x2, starting transfers between devices, local(): received = lax.all_to_all(sent, group, 0, 0, tiled=True)  12.1 us
    ppermute x4, starting transfers between devices, scan_levels(): got_gained.append(lax.ppermute(gained, axis, both_ways(pairs)))  8.08 us
  transfers between devices with their start and end apart: 9, of which 8 were waited for; matrix products, arithmetic and copies ran while one was open for 0% of the time, Pallas kernels for 1%

profile of v2, /device:TPU:13, one launch (start us, length us, event | category | flops | bytes accessed | tf_op | source)
XLA Modules:
  0.0 80.2 jit_solution(16854065425914115187)
XLA Ops:
  0.6 0.0 copy-start
  0.6 4.3 %shard_map.59 = f32[16,2,1,64,128]{4,3,2,1,0:T(8,128)} custom-call(f32[2,64,2,1024]{3,2,1,0:T(2,128)} %light_hbm.1, f32[8,128]{1,0:T(8,128)} %bitcast.2), custom_call_target="tpu_custom_call" | custom-call | tf_op jit(solution)/shard_map/pallas_call | solution.py:507
  5.0 0.0 copy-start.2
  5.0 5.4 %all-to-all-start = ((f32[16,2,1,64,128]{4,3,2,1,0:T(8,128)}), f32[16,2,1,64,128]{4,3,2,1,0:T(8,128)S(1)}, u32[]{:S(2)}, u32[]{:S(2)}) async-start(f32[16,2,1,64,128]{4,3,2,1,0:T(8,128)} %shard_map.59), calls=%async_computation | async-start | bytes 2097152 | tf_op jit(solution)/shard_map/all_to_all | solution.py:653
  10.4 0.0 copy-done
  10.4 0.1 constant_dynamic-slice_fusion.1
  10.6 0.0 copy-done.2
  10.6 0.4 shard_map.60.table_ref
  11.0 0.1 pad_maximum_fusion.density_ref
  11.1 13.0 %all-to-all-done.recv_ref = f32[16,2,1,64,128]{4,3,2,1,0:T(8,128)S(1)} async-done(((f32[16,2,1,64,128]{4,3,2,1,0:T(8,128)}), f32[16,2,1,64,128]{4,3,2,1,0:T(8,128)S(1)}, u32[]{:S(2)}, u32[]{:S(2)}) %all-to-all-start) | async-done | bytes 1048608 | tf_op jit(solution)/shard_map/all_to_all | solution.py:653
  24.1 2.5 %shard_map.61 = (f32[2,4,256,128]{3,2,1,0:T(8,128)S(1)}, f32[4,256,128]{2,1,0:T(8,128)S(1)}, f32[4,256,128]{2,1,0:T(8,128)S(1)}, f32[128,128]{1,0:T(8,128)}, f32[128,128]{1,0:T(8,128)S(1)}) custom-call(f32[16,2,1,64,128]{4,3,2,1,0:T(8,128)S(1)} %all-to-all-done.recv_ref, bf16[2,3,2,128,128]{4,3,2,1,0:T(8,128)(2,1)S(1)} %shard_map.60.table_ref, ...), custom_call_target="tpu_custom_call" | custom-call | tf_op jit(solution)/shard_map/pallas_call | solution.py:507
  26.7 2.3 %collective-permute-start = (f32[128,128]{1,0:T(8,128)S(1)}, f32[128,128]{1,0:T(8,128)S(1)}, u32[]{:S(2)}, u32[]{:S(2)}) collective-permute-start(f32[128,128]{1,0:T(8,128)S(1)} %get-tuple-element.23), channel_id=1, source_target_pairs={{0,16},{16,0},{1,17},{17,1},{2,18},{18,2},{3,19},{19,3},{4,20},{20... | collective-permute-start | bytes 196616 | tf_op jit(solution)/shard_map/ppermute | solution.py:553
  29.0 3.1 %collective-permute-done.refs_0_ = f32[128,128]{1,0:T(8,128)S(1)} collective-permute-done((f32[128,128]{1,0:T(8,128)S(1)}, f32[128,128]{1,0:T(8,128)S(1)}, u32[]{:S(2)}, u32[]{:S(2)}) %collective-permute-start) | collective-permute-done | bytes 65568 | tf_op jit(solution)/shard_map/ppermute | solution.py:553
  32.1 3.1 %shard_map.62 = (f32[16,2,1,64,128]{4,3,2,1,0:T(8,128)}, f32[8,128]{1,0:T(8,128)S(1)}) custom-call(f32[2,4,256,128]{3,2,1,0:T(8,128)S(1)} %get-tuple-element.20.field_ref, f32[4,256,128]{2,1,0:T(8,128)S(1)} %get-tuple-element.21.growth_ref, f32[4,256,128]{2,1,0:T(8,128)S(1)} %get-tuple-element.22.gained_ref, ...), custom_call_target="tpu_custom_call" | custom-call | tf_op jit(solution)/shard_map/pallas_call | solution.py:507
  35.2 0.0 copy-start.1
  35.3 6.7 %all-to-all-start.1 = ((f32[16,2,1,64,128]{4,3,2,1,0:T(8,128)}), f32[16,2,1,64,128]{4,3,2,1,0:T(8,128)}, u32[]{:S(2)}, u32[]{:S(2)}) async-start(f32[16,2,1,64,128]{4,3,2,1,0:T(8,128)} %get-tuple-element.24), calls=%async_computation.1 | async-start | bytes 2097152 | tf_op jit(solution)/shard_map/all_to_all | solution.py:670
  41.9 0.0 copy-done.1
  41.9 0.7 shard_map.63.table_ref
  42.7 13.0 %all-to-all-done.1.recv_ref = f32[16,2,1,64,128]{4,3,2,1,0:T(8,128)} async-done(((f32[16,2,1,64,128]{4,3,2,1,0:T(8,128)}), f32[16,2,1,64,128]{4,3,2,1,0:T(8,128)}, u32[]{:S(2)}, u32[]{:S(2)}) %all-to-all-start.1) | async-done | bytes 1048608 | tf_op jit(solution)/shard_map/all_to_all | solution.py:670
  55.6 2.9 %shard_map.64 = (f32[2,2,64,1024]{3,2,1,0:T(8,128)S(1)}, f32[2,64,1024]{2,1,0:T(8,128)S(1)}, f32[2,64,1024]{2,1,0:T(8,128)S(1)}, f32[2,32,1024]{2,1,0:T(8,128)S(1)}, f32[2,32,1024]{2,1,0:T(8,128)S(1)}) custom-call(f32[16,2,1,64,128]{4,3,2,1,0:T(8,128)} %all-to-all-done.1.recv_ref, bf16[8,3,2,128,128]{4,3,2,1,0:T(8,128)(2,1)S(1)} %shard_map.63.table_ref, ...), custom_call_target="tpu_custom_call" | custom-call | tf_op jit(solution)/shard_map/pallas_call | solution.py:507
  58.6 0.8 %collective-permute-start.1 = (f32[2,32,1024]{2,1,0:T(8,128)S(1)}, f32[2,32,1024]{2,1,0:T(8,128)S(1)}, u32[]{:S(2)}, u32[]{:S(2)}) collective-permute-start(f32[2,32,1024]{2,1,0:T(8,128)S(1)} %get-tuple-element.31), channel_id=1, source_target_pairs={{0,4},{4,0},{1,5},{5,1},{2,6},{6,2},{3,7},{7,3},{8,12},{12,8},{9,1... | collective-permute-start | bytes 786440 | tf_op jit(solution)/shard_map/ppermute | solution.py:685
  59.4 1.2 %collective-permute-done.1.refs_1_ = f32[2,32,1024]{2,1,0:T(8,128)S(1)} collective-permute-done((f32[2,32,1024]{2,1,0:T(8,128)S(1)}, f32[2,32,1024]{2,1,0:T(8,128)S(1)}, u32[]{:S(2)}, u32[]{:S(2)}) %collective-permute-start.1) | collective-permute-done | bytes 262176 | tf_op jit(solution)/shard_map/ppermute | solution.py:685
  60.6 0.9 %collective-permute-start.2 = (f32[32,1024]{1,0:T(8,128)S(1)}, f32[32,1024]{1,0:T(8,128)S(1)}, u32[]{:S(2)}, u32[]{:S(2)}) collective-permute-start(f32[32,1024]{1,0:T(8,128)S(1)} %get-tuple-element.32.refs_1_), channel_id=1, source_target_pairs={{0,8},{16,24},{8,0},{24,16},{1,9},{17,25},{9,1},{25,17},{2,10},{18... | collective-permute-start | bytes 393224 | tf_op jit(solution)/shard_map/ppermute | solution.py:553
  61.5 0.7 collective-permute-start.3
  62.2 3.2 %collective-permute-done.2.refs_2_ = f32[32,1024]{1,0:T(8,128)S(1)} collective-permute-done((f32[32,1024]{1,0:T(8,128)S(1)}, f32[32,1024]{1,0:T(8,128)S(1)}, u32[]{:S(2)}, u32[]{:S(2)}) %collective-permute-start.2) | collective-permute-done | bytes 131104 | tf_op jit(solution)/shard_map/ppermute | solution.py:553
  65.4 2.9 %collective-permute-start.5 = (f32[32,1024]{1,0:T(8,128)S(1)}, f32[32,1024]{1,0:T(8,128)S(1)}, u32[]{:S(2)}, u32[]{:S(2)}) collective-permute-start(f32[32,1024]{1,0:T(8,128)S(1)} %shard_map.66), channel_id=1, source_target_pairs={{8,24},{24,8},{9,25},{25,9},{10,26},{26,10},{11,27},{27,11},{12,28... | collective-permute-start | bytes 393224 | tf_op jit(solution)/shard_map/ppermute | solution.py:553
  68.3 1.9 %collective-permute-start.4 = (f32[32,1024]{1,0:T(8,128)S(1)}, f32[32,1024]{1,0:T(8,128)S(1)}, u32[]{:S(2)}, u32[]{:S(2)}) collective-permute-start(f32[32,1024]{1,0:T(8,128)S(1)} %shard_map.66), channel_id=1, source_target_pairs={{8,16},{16,8},{9,17},{17,9},{10,18},{18,10},{11,19},{19,11},{12,20... | collective-permute-start | bytes 393224 | tf_op jit(solution)/shard_map/ppermute | solution.py:553
  70.2 0.0 collective-permute-done.3.refs_3_
  70.2 1.8 %collective-permute-done.5.refs_5_ = f32[32,1024]{1,0:T(8,128)S(1)} collective-permute-done((f32[32,1024]{1,0:T(8,128)S(1)}, f32[32,1024]{1,0:T(8,128)S(1)}, u32[]{:S(2)}, u32[]{:S(2)}) %collective-permute-start.5) | collective-permute-done | bytes 131104 | tf_op jit(solution)/shard_map/ppermute | solution.py:553
  72.0 4.1 %collective-permute-done.4.refs_4_ = f32[32,1024]{1,0:T(8,128)S(1)} collective-permute-done((f32[32,1024]{1,0:T(8,128)S(1)}, f32[32,1024]{1,0:T(8,128)S(1)}, u32[]{:S(2)}, u32[]{:S(2)}) %collective-permute-start.4) | collective-permute-done | bytes 131104 | tf_op jit(solution)/shard_map/ppermute | solution.py:553
  76.1 0.1 shard_map.67
  76.2 1.1 %collective-permute-start.6 = (f32[32,1024]{1,0:T(8,128)S(1)}, f32[32,1024]{1,0:T(8,128)S(1)}, u32[]{:S(2)}, u32[]{:S(2)}) collective-permute-start(f32[32,1024]{1,0:T(8,128)S(1)} %get-tuple-element.35), channel_id=1, source_target_pairs={{0,4},{4,0},{1,5},{5,1},{2,6},{6,2},{3,7},{7,3},{8,12},{12,8},{9,1... | collective-permute-start | bytes 393224 | tf_op jit(solution)/shard_map/ppermute | solution.py:708
  77.3 1.0 %collective-permute-done.6.given_ref = f32[32,1024]{1,0:T(8,128)S(1)} collective-permute-done((f32[32,1024]{1,0:T(8,128)S(1)}, f32[32,1024]{1,0:T(8,128)S(1)}, u32[]{:S(2)}, u32[]{:S(2)}) %collective-permute-start.6) | collective-permute-done | bytes 131104 | tf_op jit(solution)/shard_map/ppermute | solution.py:708
  78.3 1.9 %shard_map.68 = (f32[2,64,2,1024]{3,2,1,0:T(2,128)}, f32[64,2,1024]{2,1,0:T(2,128)}) custom-call(f32[2,2,64,1024]{3,2,1,0:T(8,128)S(1)} %get-tuple-element.27.field_ref, f32[2,64,1024]{2,1,0:T(8,128)S(1)} %get-tuple-element.28.growth_ref, f32[2,64,1024]{2,1,0:T(8,128)S(1)} %get-tuple-element.29.gained_ref, f32[32,1024]{1,0:T(8,128)S(1)} %get-tuple-element.34.kept_ref, ...), custom_call_target="tpu_custom_call" | custom-call | tf_op jit(solution)/shard_map/pallas_call | solution.py:507
  (3 shorter events, 0.1 us)
Async XLA Ops:
  0.6 9.8 %copy-start = (f32[256,1024]{1,0:T(8,128)S(1)}, f32[256,1024]{1,0:T(8,128)}, u32[]{:S(2)}) copy-start(f32[256,1024]{1,0:T(8,128)} %param.5) | copy-start | bytes 3145732
  5.0 5.6 %copy-start.2 = (f32[256]{0:T(256)S(1)}, f32[256]{0:T(256)}, u32[]{:S(2)}) copy-start(f32[256]{0:T(256)} %param.6) | copy-start | bytes 3076
  5.0 19.1 %all-to-all-start = ((f32[16,2,1,64,128]{4,3,2,1,0:T(8,128)}), f32[16,2,1,64,128]{4,3,2,1,0:T(8,128)S(1)}, u32[]{:S(2)}, u32[]{:S(2)}) async-start(f32[16,2,1,64,128]{4,3,2,1,0:T(8,128)} %shard_map.59), calls=%async_computation | async-start | bytes 2097152 | tf_op jit(solution)/shard_map/all_to_all | solution.py:653
  26.7 5.5 %collective-permute-start = (f32[128,128]{1,0:T(8,128)S(1)}, f32[128,128]{1,0:T(8,128)S(1)}, u32[]{:S(2)}, u32[]{:S(2)}) collective-permute-start(f32[128,128]{1,0:T(8,128)S(1)} %get-tuple-element.23), channel_id=1, source_target_pairs={{0,16},{16,0},{1,17},{17,1},{2,18},{18,2},{3,19},{19,3},{4,20},{20... | collective-permute-start | bytes 196616 | tf_op jit(solution)/shard_map/ppermute | solution.py:553
  35.2 6.7 %copy-start.1 = (f32[1024]{0:T(1024)S(1)}, f32[1024]{0:T(1024)}, u32[]{:S(2)}) copy-start(f32[1024]{0:T(1024)} %param.7) | copy-start | bytes 12292
  35.3 20.4 %all-to-all-start.1 = ((f32[16,2,1,64,128]{4,3,2,1,0:T(8,128)}), f32[16,2,1,64,128]{4,3,2,1,0:T(8,128)}, u32[]{:S(2)}, u32[]{:S(2)}) async-start(f32[16,2,1,64,128]{4,3,2,1,0:T(8,128)} %get-tuple-element.24), calls=%async_computation.1 | async-start | bytes 2097152 | tf_op jit(solution)/shard_map/all_to_all | solution.py:670
  58.6 2.0 %collective-permute-start.1 = (f32[2,32,1024]{2,1,0:T(8,128)S(1)}, f32[2,32,1024]{2,1,0:T(8,128)S(1)}, u32[]{:S(2)}, u32[]{:S(2)}) collective-permute-start(f32[2,32,1024]{2,1,0:T(8,128)S(1)} %get-tuple-element.31), channel_id=1, source_target_pairs={{0,4},{4,0},{1,5},{5,1},{2,6},{6,2},{3,7},{7,3},{8,12},{12,8},{9,1... | collective-permute-start | bytes 786440 | tf_op jit(solution)/shard_map/ppermute | solution.py:685
  60.6 4.7 %collective-permute-start.2 = (f32[32,1024]{1,0:T(8,128)S(1)}, f32[32,1024]{1,0:T(8,128)S(1)}, u32[]{:S(2)}, u32[]{:S(2)}) collective-permute-start(f32[32,1024]{1,0:T(8,128)S(1)} %get-tuple-element.32.refs_1_), channel_id=1, source_target_pairs={{0,8},{16,24},{8,0},{24,16},{1,9},{17,25},{9,1},{25,17},{2,10},{18... | collective-permute-start | bytes 393224 | tf_op jit(solution)/shard_map/ppermute | solution.py:553
  61.5 8.7 %collective-permute-start.3 = (f32[32,1024]{1,0:T(8,128)S(1)}, f32[32,1024]{1,0:T(8,128)S(1)}, u32[]{:S(2)}, u32[]{:S(2)}) collective-permute-start(f32[32,1024]{1,0:T(8,128)S(1)} %get-tuple-element.33.refs_0_), channel_id=1, source_target_pairs={{16,24},{24,16},{17,25},{25,17},{18,26},{26,18},{19,27},{27,19},{2... | collective-permute-start | bytes 393224 | tf_op jit(solution)/shard_map/ppermute | solution.py:556
  65.4 6.6 %collective-permute-start.5 = (f32[32,1024]{1,0:T(8,128)S(1)}, f32[32,1024]{1,0:T(8,128)S(1)}, u32[]{:S(2)}, u32[]{:S(2)}) collective-permute-start(f32[32,1024]{1,0:T(8,128)S(1)} %shard_map.66), channel_id=1, source_target_pairs={{8,24},{24,8},{9,25},{25,9},{10,26},{26,10},{11,27},{27,11},{12,28... | collective-permute-start | bytes 393224 | tf_op jit(solution)/shard_map/ppermute | solution.py:553
  68.3 7.8 %collective-permute-start.4 = (f32[32,1024]{1,0:T(8,128)S(1)}, f32[32,1024]{1,0:T(8,128)S(1)}, u32[]{:S(2)}, u32[]{:S(2)}) collective-permute-start(f32[32,1024]{1,0:T(8,128)S(1)} %shard_map.66), channel_id=1, source_target_pairs={{8,16},{16,8},{9,17},{17,9},{10,18},{18,10},{11,19},{19,11},{12,20... | collective-permute-start | bytes 393224 | tf_op jit(solution)/shard_map/ppermute | solution.py:553
  76.2 2.1 %collective-permute-start.6 = (f32[32,1024]{1,0:T(8,128)S(1)}, f32[32,1024]{1,0:T(8,128)S(1)}, u32[]{:S(2)}, u32[]{:S(2)}) collective-permute-start(f32[32,1024]{1,0:T(8,128)S(1)} %get-tuple-element.35), channel_id=1, source_target_pairs={{0,4},{4,0},{1,5},{5,1},{2,6},{6,2},{3,7},{7,3},{8,12},{12,8},{9,1... | collective-permute-start | bytes 393224 | tf_op jit(solution)/shard_map/ppermute | solution.py:708

commit v3 on v2

--- a/solution.py
+++ b/solution.py
@@ -17,8 +17,8 @@
 PLASMA = 4.0
 LANES = 128
 HALF = LANES // 2
+Z_AXES = ("zh", "zl")
 GROUP = {True: ("zl", "core", "trans"), False: ("core", "trans")}
-LATER = {True: ("zh",), False: ("zh", "zl")}
 VMEM_LIMIT = 16 * 1024 * 1024
 F32 = jnp.float32
 BF16 = jnp.bfloat16
@@ -204,12 +204,14 @@
     width = send_ref.shape[-1]
     step = min(16, across)
     chunks = range(0, across, step)
-    phase_copy = pltpu.make_async_copy(phase_hbm, phase_ref, sem.at[0])
+    count = send_ref.shape[0] // 2
+    flip = lax.rem(lax.axis_index("zh"), 2) if packed else 0
+    phase_copy = pltpu.make_async_copy(phase_hbm, phase_ref, sem.at[0, 0])
     phase_copy.start()
     arriving = []
     for i, x in enumerate(chunks):
         rows = pl.ds(x, step)
-        copy = pltpu.make_async_copy(light_hbm.at[:, rows], light_ref.at[:, rows], sem.at[1 + i])
+        copy = pltpu.make_async_copy(light_hbm.at[:, rows], light_ref.at[:, rows], sem.at[1 + i, 0])
         copy.start()
         arriving.append(copy)
     phase_copy.wait()
@@ -253,11 +255,14 @@
                                 lanes = slice(piece * width, (piece + 1) * width)
                                 send_ref[slab, c, t, rows, :] = values[t][:, lanes]
         rows = pl.ds(begin, step)
-        copy = pltpu.make_async_copy(
-            send_ref.at[:, :, :, rows], send_hbm.at[:, :, :, rows], sem.at[1 + i]
-        )
-        copy.start()
-        leaving.append(copy)
+        for j in range(2):
+            slabs = pl.ds(j * count, count)
+            places = pl.ds(lax.rem(flip + j, 2) * count, count)
+            copy = pltpu.make_async_copy(
+                send_ref.at[slabs, :, :, rows], send_hbm.at[places, :, :, rows], sem.at[1 + i, j]
+            )
+            copy.start()
+            leaving.append(copy)
     for copy in leaving:
         copy.wait()
 
@@ -350,17 +355,16 @@
 
 def third_kernel(packed, rebuild, leaves, field_ref, growth_ref, gained_ref, table_ref, *refs):
     got_refs = refs[:leaves]
-    send_hbm, token_ref, parts_ref, mid_ref, send_ref, sem = refs[leaves:]
+    send_hbm, parts_ref, mid_ref, send_ref, sem = refs[leaves:]
 
     def enter(start, step):
         got = [ref[start : start + step, :] for ref in got_refs]
-        return finish_scan(LATER[packed], rebuild(got))
+        return finish_scan(Z_AXES, rebuild(got), packed)
 
     radix = table_ref.shape[0]
     _, total, _, width = field_ref.shape
     slabs, _, times, across, _ = send_ref.shape
     trans = (radix * LANES) // across
-    token_ref[...] = jnp.zeros_like(token_ref)
     step = 16
     upper = upper_lanes((step, LANES))
     for start in range(0, LANES, step):
@@ -412,11 +416,14 @@
     core = lax.axis_index("core")
     step = min(16, across)
     upper = upper_lanes((step, LANES))
+    slabs = recv_ref.shape[0]
+    flip = lax.rem(lax.axis_index("zh"), 2) * (slabs // 2) if packed else 0
 
     def part(c, t, x, a):
         rows = slice(x, x + step)
         if packed:
-            one, two = recv_ref[2 * a, c, 0, rows, :], recv_ref[2 * a + 1, c, 0, rows, :]
+            place = lax.rem(2 * a + flip, slabs)
+            one, two = recv_ref[place, c, 0, rows, :], recv_ref[place + 1, c, 0, rows, :]
             if t == 0:
                 return jnp.where(upper, swap_halves(two), one)
             return jnp.where(upper, two, swap_halves(one))
@@ -466,39 +473,54 @@
     pl.when(core == 1)(functools.partial(hand_out, 1))
 
 
-def fifth_kernel(
-    field_ref, growth_ref, gained_ref, kept_ref, given_ref, light_hbm, electrons_hbm, light_ref, electrons_ref, sem
+def turn_rows(base, x, field_ref, growth_ref, gained_ref, entering_ref, light_ref, electrons_ref):
+    _, times, _, length = field_ref.shape
+    rows, out_rows = pl.ds(pl.multiple_of(base + x, 8), 8), slice(x, x + 8)
+    entering = entering_ref[out_rows, :]
+    for t in range(times):
+        results = []
+        for a in range(length // LANES):
+            lanes = slice(a * LANES, (a + 1) * LANES)
+            electrons = growth_ref[t, rows, lanes] * entering[:, lanes] + gained_ref[t, rows, lanes]
+            re, im = rotate(field_ref[0, t, rows, lanes], field_ref[1, t, rows, lanes], electrons)
+            results.append((re, im, electrons))
+        re, im, electrons = (jnp.concatenate(part, axis=1) for part in zip(*results, strict=True))
+        light_ref[0, out_rows, t, :] = re
+        light_ref[1, out_rows, t, :] = im
+        electrons_ref[out_rows, t, :] = electrons
+
+
+def own_kernel(field_ref, growth_ref, gained_ref, entering_ref, light_ref, electrons_ref):
+    half = field_ref.shape[2] // 2
+    base = lax.axis_index("core") * half
+    for x in range(0, half, 8):
+        turn_rows(base, x, field_ref, growth_ref, gained_ref, entering_ref, light_ref, electrons_ref)
+
+
+def other_kernel(
+    field_ref, growth_ref, gained_ref, entering_ref, own_light_ref, own_electrons_ref, light_hbm, electrons_hbm,
+    light_ref, electrons_ref, sem,
 ):
-    _, times, across, length = field_ref.shape
-    half = across // 2
+    half = field_ref.shape[2] // 2
     core = lax.axis_index("core")
-    step = min(16, half)
+    base = (1 - core) * half
     leaving = []
-    for i, begin in enumerate(range(0, across, step)):
-        for x in range(begin, begin + step, 8):
-            own, row = x // half, x % half
-            rows = slice(x, x + 8)
-            entering = jnp.where(core == own, kept_ref[row : row + 8, :], given_ref[row : row + 8, :])
-            for t in range(times):
-                results = []
-                for a in range(length // LANES):
-                    lanes = slice(a * LANES, (a + 1) * LANES)
-                    electrons = (
-                        growth_ref[t, rows, lanes] * entering[:, lanes] + gained_ref[t, rows, lanes]
-                    )
-                    re, im = rotate(field_ref[0, t, rows, lanes], field_ref[1, t, rows, lanes], electrons)
-                    results.append((re, im, electrons))
-                re, im, electrons = (jnp.concatenate(part, axis=1) for part in zip(*results, strict=True))
-                light_ref[0, rows, t, :] = re
-                light_ref[1, rows, t, :] = im
-                electrons_ref[rows, t, :] = electrons
-        block = pl.ds(begin, step)
+
+    def leave(i, light, electrons, target):
         for copy in (
-            pltpu.make_async_copy(light_ref.at[:, block], light_hbm.at[:, block], sem.at[0, i]),
-            pltpu.make_async_copy(electrons_ref.at[block], electrons_hbm.at[block], sem.at[1, i]),
+            pltpu.make_async_copy(light, light_hbm.at[:, target], sem.at[0, i]),
+            pltpu.make_async_copy(electrons, electrons_hbm.at[target], sem.at[1, i]),
         ):
             copy.start()
             leaving.append(copy)
+
+    leave(0, own_light_ref, own_electrons_ref, pl.ds(core * half, half))
+    step = min(8, half)
+    for i, begin in enumerate(range(0, half, step)):
+        for x in range(begin, begin + step, 8):
+            turn_rows(base, x, field_ref, growth_ref, gained_ref, entering_ref, light_ref, electrons_ref)
+        block = pl.ds(begin, step)
+        leave(1 + i, light_ref.at[:, block], electrons_ref.at[block], pl.ds(base + begin, step))
     for copy in leaving:
         copy.wait()
 
@@ -537,8 +559,12 @@
     return pairs + [(b, a) for a, b in pairs]
 
 
-def scan_levels(axis, growth, gained):
-    count = lax.axis_size(axis)
+def widen(pairs):
+    return [(2 * a + i, 2 * b + (i + a + b) % 2) for a, b in pairs for i in range(2)]
+
+
+def scan_levels(axis, growth, gained, paired):
+    count = lax.axis_size(axis) // (2 if paired else 1)
     kept = []
     size = 1
     while size < count:
@@ -550,10 +576,11 @@
                 for b in range(0, count, 2 * size)
                 if b + size - 1 + reach < count
             ]
-            got_gained.append(lax.ppermute(gained, axis, both_ways(pairs)))
+            spread = widen if paired else list
+            got_gained.append(lax.ppermute(gained, axis, spread(both_ways(pairs))))
             if need_growth:
                 later = [pair for pair in pairs if pair[0] >= 2 * size]
-                got_growth.append(lax.ppermute(growth, axis, both_ways(later)))
+                got_growth.append(lax.ppermute(growth, axis, spread(both_ways(later))))
         kept.append((got_gained, got_growth))
         if need_growth and 4 * size < count:
 
@@ -570,8 +597,8 @@
     return kept
 
 
-def finish_scan(axis, levels):
-    place = lax.axis_index(axis)
+def finish_scan(axis, levels, paired):
+    place = lax.axis_index(axis) // (2 if paired else 1)
     before_growth = before_gained = None
     for level, (got_gained, got_growth) in enumerate(levels):
         new_gained = sum(got_gained)
@@ -600,11 +627,11 @@
     radix_x, radix_y = width_x // LANES, width_y // LANES
     _, across, times, _ = light_field.shape
     group = GROUP[packed]
-    later = LATER[packed]
-    whole = ("zh", "zl")
     slabs = lax.axis_size(group)
     width = width_y // slabs
     slab = lax.axis_index(group)
+    if packed:
+        slab = lax.rem(slab + lax.rem(lax.axis_index("zh"), 2) * (slabs // 2), slabs)
     trans = lax.axis_size("trans")
     density_y = lax.dynamic_slice_in_dim(gas_density, slab * width, width, 1)
     density_x = lax.dynamic_slice_in_dim(gas_density, lax.axis_index("trans") * across, across, 0)
@@ -647,7 +674,7 @@
             pltpu.VMEM((2, times, across, width_y), F32),
             pltpu.VMEM(phase_y.shape, F32),
             pltpu.VMEM(sent_shape, F32),
-            pltpu.SemaphoreType.DMA((1 + across // min(16, across),)),
+            pltpu.SemaphoreType.DMA((1 + across // min(16, across), 2)),
         ],
     )
     received = lax.all_to_all(sent, group, 0, 0, tiled=True)
@@ -659,20 +686,21 @@
         vmem((2, total) + cells, (total,) + cells, (total,) + cells, last, last),
         scratch_x,
     )
-    levels = scan_levels(later, last_growth, last_gained)
+    levels = scan_levels(Z_AXES, last_growth, last_gained, packed)
     leaves, rebuild = flatten(levels)
-    sent, token = call(
+    (table_y,) = call(
+        functools.partial(table_kernel, 1),
+        [(phase_y, VMEM_SPEC), (last_gained, VMEM_SPEC)],
+        [(table_y_shape, BF16, VMEM_SPEC)],
+    )
+    table_y, leaves = lax.optimization_barrier((table_y, leaves))
+    (sent,) = call(
         functools.partial(third_kernel, packed, rebuild, len(leaves)),
         [(array, VMEM_SPEC) for array in (field, growth, gained, table_x, *leaves)],
-        [(sent_shape, F32, HBM_SPEC), ((8, LANES), F32, VMEM_SPEC)],
+        [(sent_shape, F32, HBM_SPEC)],
         scratch_x + [pltpu.VMEM(sent_shape, F32), pltpu.SemaphoreType.DMA((slabs // trans,))],
     )
     received = lax.all_to_all(sent, group, 0, 0, tiled=True)
-    (table_y,) = call(
-        functools.partial(table_kernel, 1),
-        [(phase_y, VMEM_SPEC), (token, VMEM_SPEC)],
-        [(table_y_shape, BF16, VMEM_SPEC)],
-    )
     cells = (across, width_y)
     half = (2, across // 2, width_y)
     field, growth, gained, mine, theirs = call(
@@ -694,27 +722,30 @@
         early, late = ordered(mine, other)
         return late[0] * early[0], late[0] * early[1] + late[1]
 
-    levels = scan_levels(whole, *fuse(chip_map, mine, other))
+    levels = scan_levels(Z_AXES, *fuse(chip_map, mine, other), False)
     leaves, rebuild = flatten(levels)
 
     def hand_over(mine, other, *got):
         early, _ = ordered(mine, other)
         first = lax.axis_index("core") == 0
-        entering = finish_scan(whole, rebuild(got))
+        entering = finish_scan(Z_AXES, rebuild(got), False)
         halfway = early[0] * entering + early[1]
         return jnp.where(first, entering, halfway), jnp.where(first, halfway, entering)
 
     kept, given = fuse(hand_over, mine, other, *leaves)
     given = lax.ppermute(given, "core", swap)
-    chunks = across // min(16, across // 2)
+    rows = across // 2
+    operands = [(array, VMEM_SPEC) for array in (field, growth, gained)]
+    light_half, electrons_half = (2, rows, times, width_y), (rows, times, width_y)
+    own = call(own_kernel, operands + [(kept, VMEM_SPEC)], vmem(light_half, electrons_half))
     return call(
-        fifth_kernel,
-        [(array, VMEM_SPEC) for array in (field, growth, gained, kept, given)],
+        other_kernel,
+        operands + [(array, VMEM_SPEC) for array in (given, *own)],
         [(light_field.shape, F32, HBM_SPEC), ((across, times, width_y), F32, HBM_SPEC)],
         [
-            pltpu.VMEM(light_field.shape, F32),
-            pltpu.VMEM((across, times, width_y), F32),
-            pltpu.SemaphoreType.DMA((2, chunks)),
+            pltpu.VMEM(light_half, F32),
+            pltpu.VMEM(electrons_half, F32),
+            pltpu.SemaphoreType.DMA((2, 1 + rows // min(8, rows))),
         ],
     )
 

time: 80.6 us -> 77.1 us (0.957)
  the two profiles are of different devices: /device:TPU:13 before, /device:TPU:17 now
where the time goes in v3:
time: 77.1 us; the launch traced here: 76.2 us
  waiting for transfers between devices  24.3 us (32%)
  blocking collectives  20.9 us (27%)
  starting transfers between devices  15.7 us (20%)
  Pallas kernels  14.2 us (18%)
  between operations  0.82 us (1%)
    all_to_all x1, blocking collectives, local(): received = lax.all_to_all(sent, group, 0, 0, tiled=True)  20.9 us
    pallas_call x11, Pallas kernels, call(): pl.pallas_call(kernel, out_shape=[jax.ShapeDtypeStruct(shape, kind) for s...  14.2 us
    all_to_all x1, waiting for transfers between devices, local(): received = lax.all_to_all(sent, group, 0, 0, tiled=True)  14.1 us
    ppermute x4, waiting for transfers between devices, scan_levels(): got_gained.append(lax.ppermute(gained, axis, spread(both_ways(pairs))))  8.27 us
    ppermute x4, starting transfers between devices, scan_levels(): got_gained.append(lax.ppermute(gained, axis, spread(both_ways(pairs))))  5.71 us
    all_to_all x1, starting transfers between devices, local(): received = lax.all_to_all(sent, group, 0, 0, tiled=True)  5.44 us
    ppermute x1, starting transfers between devices, scan_levels(): got_growth.append(lax.ppermute(growth, axis, spread(both_ways(later))))  3.04 us
  transfers between devices with their start and end apart: 8, of which 6 were waited for; matrix products, arithmetic and copies ran while one was open for 0% of the time, Pallas kernels for 2%

profile of v3, /device:TPU:17, one launch (start us, length us, event | category | flops | bytes accessed | tf_op | source)
XLA Modules:
  0.0 76.2 jit_solution(14829606316689277931)
XLA Ops:
  0.6 0.0 copy-start
  0.6 4.4 %shard_map.59 = f32[16,2,1,64,128]{4,3,2,1,0:T(8,128)} custom-call(f32[2,64,2,1024]{3,2,1,0:T(2,128)} %light_hbm.1, f32[8,128]{1,0:T(8,128)} %bitcast.2), custom_call_target="tpu_custom_call" | custom-call | tf_op jit(solution)/shard_map/pallas_call | solution.py:529
  5.0 0.0 copy-start.2
  5.0 5.4 %all-to-all-start = ((f32[16,2,1,64,128]{4,3,2,1,0:T(8,128)}), f32[16,2,1,64,128]{4,3,2,1,0:T(8,128)S(1)}, u32[]{:S(2)}, u32[]{:S(2)}) async-start(f32[16,2,1,64,128]{4,3,2,1,0:T(8,128)} %shard_map.59), calls=%async_computation | async-start | bytes 2097152 | tf_op jit(solution)/shard_map/all_to_all | solution.py:680
  10.5 0.0 copy-start.1
  10.5 0.0 copy-done
  10.5 0.1 constant_dynamic-slice_fusion.1
  10.7 0.0 copy-done.2
  10.7 0.4 shard_map.60.table_ref
  11.1 0.1 pad_maximum_fusion.density_ref
  11.2 14.1 %all-to-all-done.recv_ref = f32[16,2,1,64,128]{4,3,2,1,0:T(8,128)S(1)} async-done(((f32[16,2,1,64,128]{4,3,2,1,0:T(8,128)}), f32[16,2,1,64,128]{4,3,2,1,0:T(8,128)S(1)}, u32[]{:S(2)}, u32[]{:S(2)}) %all-to-all-start) | async-done | bytes 1048608 | tf_op jit(solution)/shard_map/all_to_all | solution.py:680
  25.3 2.5 %shard_map.61 = (f32[2,4,256,128]{3,2,1,0:T(8,128)S(1)}, f32[4,256,128]{2,1,0:T(8,128)S(1)}, f32[4,256,128]{2,1,0:T(8,128)S(1)}, f32[128,128]{1,0:T(8,128)}, f32[128,128]{1,0:T(8,128)S(1)}) custom-call(f32[16,2,1,64,128]{4,3,2,1,0:T(8,128)S(1)} %all-to-all-done.recv_ref, bf16[2,3,2,128,128]{4,3,2,1,0:T(8,128)(2,1)S(1)} %shard_map.60.table_ref, ...), custom_call_target="tpu_custom_call" | custom-call | tf_op jit(solution)/shard_map/pallas_call | solution.py:529
  27.9 0.0 collective-permute-start
  27.9 0.0 copy-done.1
  27.9 0.7 shard_map.62.table_ref
  28.6 2.7 %collective-permute-done.refs_0_ = f32[128,128]{1,0:T(8,128)S(1)} collective-permute-done((f32[128,128]{1,0:T(8,128)S(1)}, f32[128,128]{1,0:T(8,128)S(1)}, u32[]{:S(2)}, u32[]{:S(2)}) %collective-permute-start) | collective-permute-done | bytes 65568 | tf_op jit(solution)/shard_map/ppermute | solution.py:580
  31.3 2.4 %shard_map.63 = f32[16,2,1,64,128]{4,3,2,1,0:T(8,128)S(1)} custom-call(f32[2,4,256,128]{3,2,1,0:T(8,128)S(1)} %get-tuple-element.22.field_ref, f32[4,256,128]{2,1,0:T(8,128)S(1)} %get-tuple-element.23.growth_ref, f32[4,256,128]{2,1,0:T(8,128)S(1)} %get-tuple-element.24.gained_ref, bf16[2,3,2,128,128]{4,3,2,1,0:T(8,128)(2,1)S(1)} %shard_map.60.table_ref, ...), custom_call_target="tpu_custom_call" | custom-call | tf_op jit(solution)/shard_map/pallas_call | solution.py:529
  33.7 20.9 %all_to_all.10.recv_ref = f32[16,2,1,64,128]{4,3,2,1,0:T(8,128)S(1)} all-to-all(f32[16,2,1,64,128]{4,3,2,1,0:T(8,128)S(1)} %shard_map.63), channel_id=1, replica_groups=mesh['zh'=2,'zl'=2,'core'=2,'trans'=4] {'zl','core','trans'}, dimensions={0} | all-to-all | bytes 2097152 | tf_op jit(solution)/shard_map/all_to_all | solution.py:703
  54.7 1.7 %shard_map.64 = (f32[2,2,64,1024]{3,2,1,0:T(8,128)S(1)}, f32[2,64,1024]{2,1,0:T(8,128)S(1)}, f32[2,64,1024]{2,1,0:T(8,128)S(1)}, f32[2,32,1024]{2,1,0:T(8,128)S(1)}, f32[2,32,1024]{2,1,0:T(8,128)S(1)}) custom-call(f32[16,2,1,64,128]{4,3,2,1,0:T(8,128)S(1)} %all_to_all.10.recv_ref, bf16[8,3,2,128,128]{4,3,2,1,0:T(8,128)(2,1)S(1)} %shard_map.62.table_ref, ...), custom_call_target="tpu_custom_call" | custom-call | tf_op jit(solution)/shard_map/pallas_call | solution.py:529
  56.4 0.1 collective-permute-start.1
  56.5 1.5 %collective-permute-done.1.refs_1_ = f32[2,32,1024]{2,1,0:T(8,128)S(1)} collective-permute-done((f32[2,32,1024]{2,1,0:T(8,128)S(1)}, f32[2,32,1024]{2,1,0:T(8,128)S(1)}, u32[]{:S(2)}, u32[]{:S(2)}) %collective-permute-start.1) | collective-permute-done | bytes 262176 | tf_op jit(solution)/shard_map/ppermute | solution.py:713
  58.0 0.4 collective-permute-start.2
  58.4 3.0 %collective-permute-start.3 = (f32[32,1024]{1,0:T(8,128)S(1)}, f32[32,1024]{1,0:T(8,128)S(1)}, u32[]{:S(2)}, u32[]{:S(2)}) collective-permute-start(f32[32,1024]{1,0:T(8,128)S(1)} %get-tuple-element.35.refs_0_), channel_id=1, source_target_pairs={{16,24},{24,16},{17,25},{25,17},{18,26},{26,18},{19,27},{27,19},{2... | collective-permute-start | bytes 393224 | tf_op jit(solution)/shard_map/ppermute | solution.py:583
  61.5 1.5 %collective-permute-done.2.refs_2_ = f32[32,1024]{1,0:T(8,128)S(1)} collective-permute-done((f32[32,1024]{1,0:T(8,128)S(1)}, f32[32,1024]{1,0:T(8,128)S(1)}, u32[]{:S(2)}, u32[]{:S(2)}) %collective-permute-start.2) | collective-permute-done | bytes 131104 | tf_op jit(solution)/shard_map/ppermute | solution.py:580
  63.0 0.7 collective-permute-start.5
  63.7 4.6 %collective-permute-start.4 = (f32[32,1024]{1,0:T(8,128)S(1)}, f32[32,1024]{1,0:T(8,128)S(1)}, u32[]{:S(2)}, u32[]{:S(2)}) collective-permute-start(f32[32,1024]{1,0:T(8,128)S(1)} %shard_map.66), channel_id=1, source_target_pairs={{8,16},{16,8},{9,17},{17,9},{10,18},{18,10},{11,19},{19,11},{12,20... | collective-permute-start | bytes 393224 | tf_op jit(solution)/shard_map/ppermute | solution.py:580
  68.4 0.0 collective-permute-done.3.refs_3_
  68.4 0.0 collective-permute-done.5.refs_5_
  68.4 4.0 %collective-permute-done.4.refs_4_ = f32[32,1024]{1,0:T(8,128)S(1)} collective-permute-done((f32[32,1024]{1,0:T(8,128)S(1)}, f32[32,1024]{1,0:T(8,128)S(1)}, u32[]{:S(2)}, u32[]{:S(2)}) %collective-permute-start.4) | collective-permute-done | bytes 131104 | tf_op jit(solution)/shard_map/ppermute | solution.py:580
  72.4 0.1 shard_map.67
  72.5 1.4 %collective-permute-start.6 = (f32[32,1024]{1,0:T(8,128)S(1)}, f32[32,1024]{1,0:T(8,128)S(1)}, u32[]{:S(2)}, u32[]{:S(2)}) collective-permute-start(f32[32,1024]{1,0:T(8,128)S(1)} %get-tuple-element.36), channel_id=1, source_target_pairs={{0,4},{4,0},{1,5},{5,1},{2,6},{6,2},{3,7},{7,3},{8,12},{12,8},{9,1... | collective-permute-start | bytes 393224 | tf_op jit(solution)/shard_map/ppermute | solution.py:736
  73.9 0.5 shard_map.68
  74.4 0.4 collective-permute-done.6.entering_ref
  74.9 1.3 %shard_map.69 = (f32[2,64,2,1024]{3,2,1,0:T(2,128)}, f32[64,2,1024]{2,1,0:T(2,128)}) custom-call(f32[2,2,64,1024]{3,2,1,0:T(8,128)S(1)} %get-tuple-element.29.field_ref, f32[2,64,1024]{2,1,0:T(8,128)S(1)} %get-tuple-element.30.growth_ref, f32[2,64,1024]{2,1,0:T(8,128)S(1)} %get-tuple-element.31.gained_ref, ...), custom_call_target="tpu_custom_call" | custom-call | tf_op jit(solution)/shard_map/pallas_call | solution.py:529
  (3 shorter events, 0.1 us)
Async XLA Ops:
  0.6 9.9 %copy-start = (f32[256,1024]{1,0:T(8,128)S(1)}, f32[256,1024]{1,0:T(8,128)}, u32[]{:S(2)}) copy-start(f32[256,1024]{1,0:T(8,128)} %param.5) | copy-start | bytes 3145732
  5.0 5.6 %copy-start.2 = (f32[256]{0:T(256)S(1)}, f32[256]{0:T(256)}, u32[]{:S(2)}) copy-start(f32[256]{0:T(256)} %param.6) | copy-start | bytes 3076
  5.0 20.3 %all-to-all-start = ((f32[16,2,1,64,128]{4,3,2,1,0:T(8,128)}), f32[16,2,1,64,128]{4,3,2,1,0:T(8,128)S(1)}, u32[]{:S(2)}, u32[]{:S(2)}) async-start(f32[16,2,1,64,128]{4,3,2,1,0:T(8,128)} %shard_map.59), calls=%async_computation | async-start | bytes 2097152 | tf_op jit(solution)/shard_map/all_to_all | solution.py:680
  10.5 17.4 %copy-start.1 = (f32[1024]{0:T(1024)S(1)}, f32[1024]{0:T(1024)}, u32[]{:S(2)}) copy-start(f32[1024]{0:T(1024)} %param.7) | copy-start | bytes 12292
  27.9 3.4 %collective-permute-start = (f32[128,128]{1,0:T(8,128)S(1)}, f32[128,128]{1,0:T(8,128)S(1)}, u32[]{:S(2)}, u32[]{:S(2)}) collective-permute-start(f32[128,128]{1,0:T(8,128)S(1)} %get-tuple-element.25.refs_0_), channel_id=1, source_target_pairs={{0,24},{8,16},{16,8},{24,0},{1,25},{9,17},{17,9},{25,1},{2,26},{10... | collective-permute-start | bytes 196616 | tf_op jit(solution)/shard_map/ppermute | solution.py:580
  56.4 1.6 %collective-permute-start.1 = (f32[2,32,1024]{2,1,0:T(8,128)S(1)}, f32[2,32,1024]{2,1,0:T(8,128)S(1)}, u32[]{:S(2)}, u32[]{:S(2)}) collective-permute-start(f32[2,32,1024]{2,1,0:T(8,128)S(1)} %get-tuple-element.33), channel_id=1, source_target_pairs={{0,4},{4,0},{1,5},{5,1},{2,6},{6,2},{3,7},{7,3},{8,12},{12,8},{9,1... | collective-permute-start | bytes 786440 | tf_op jit(solution)/shard_map/ppermute | solution.py:713
  58.0 5.0 %collective-permute-start.2 = (f32[32,1024]{1,0:T(8,128)S(1)}, f32[32,1024]{1,0:T(8,128)S(1)}, u32[]{:S(2)}, u32[]{:S(2)}) collective-permute-start(f32[32,1024]{1,0:T(8,128)S(1)} %get-tuple-element.34.refs_1_), channel_id=1, source_target_pairs={{0,8},{16,24},{8,0},{24,16},{1,9},{17,25},{9,1},{25,17},{2,10},{18... | collective-permute-start | bytes 393224 | tf_op jit(solution)/shard_map/ppermute | solution.py:580
  58.4 10.0 %collective-permute-start.3 = (f32[32,1024]{1,0:T(8,128)S(1)}, f32[32,1024]{1,0:T(8,128)S(1)}, u32[]{:S(2)}, u32[]{:S(2)}) collective-permute-start(f32[32,1024]{1,0:T(8,128)S(1)} %get-tuple-element.35.refs_0_), channel_id=1, source_target_pairs={{16,24},{24,16},{17,25},{25,17},{18,26},{26,18},{19,27},{27,19},{2... | collective-permute-start | bytes 393224 | tf_op jit(solution)/shard_map/ppermute | solution.py:583
  63.0 5.3 %collective-permute-start.5 = (f32[32,1024]{1,0:T(8,128)S(1)}, f32[32,1024]{1,0:T(8,128)S(1)}, u32[]{:S(2)}, u32[]{:S(2)}) collective-permute-start(f32[32,1024]{1,0:T(8,128)S(1)} %shard_map.66), channel_id=1, source_target_pairs={{8,24},{24,8},{9,25},{25,9},{10,26},{26,10},{11,27},{27,11},{12,28... | collective-permute-start | bytes 393224 | tf_op jit(solution)/shard_map/ppermute | solution.py:580
  63.7 8.7 %collective-permute-start.4 = (f32[32,1024]{1,0:T(8,128)S(1)}, f32[32,1024]{1,0:T(8,128)S(1)}, u32[]{:S(2)}, u32[]{:S(2)}) collective-permute-start(f32[32,1024]{1,0:T(8,128)S(1)} %shard_map.66), channel_id=1, source_target_pairs={{8,16},{16,8},{9,17},{17,9},{10,18},{18,10},{11,19},{19,11},{12,20... | collective-permute-start | bytes 393224 | tf_op jit(solution)/shard_map/ppermute | solution.py:580
  72.5 2.4 %collective-permute-start.6 = (f32[32,1024]{1,0:T(8,128)S(1)}, f32[32,1024]{1,0:T(8,128)S(1)}, u32[]{:S(2)}, u32[]{:S(2)}) collective-permute-start(f32[32,1024]{1,0:T(8,128)S(1)} %get-tuple-element.36), channel_id=1, source_target_pairs={{0,4},{4,0},{1,5},{5,1},{2,6},{6,2},{3,7},{7,3},{8,12},{12,8},{9,1... | collective-permute-start | bytes 393224 | tf_op jit(solution)/shard_map/ppermute | solution.py:736
